TPU v7x, 32 devices: a whole 2x2x4 slice. The times are simulated.
32 devices in a mesh: dp: 16 (over z, x, core), tp: 2 (over y).
Axes of the slice: x: 2, y: 2, z: 4, core: 2. Of those that a mesh axis runs over, the one named last changes fastest.
Arguments:
- q_nope: bfloat16 [512, 2048], P('dp', 'tp'), may hold values from -4 to 4
- q_rope: bfloat16 [512, 1024], P('dp', 'tp'), may hold values from -80 to 80
- lengths: int32 [512], P('dp'), may hold values from 1 to 512, as said below
- page_table: int32 [512, 8], P('dp'), may hold values from 0 to 95, as said below
- lend_counts: int32 [512, 2], P('dp'), may hold values from 0 to 2, as said below
- latent_pages: bfloat16 [1536, 64, 512], P('dp'), may hold values from -5 to 5
- rope_pages: bfloat16 [1536, 4096], P('dp'), may hold values from -4 to 4
- w_uk: bfloat16 [16, 128, 512], P('tp'), may hold values from -0.5 to 0.5
- w_uv: bfloat16 [16, 512, 128], P('tp'), may hold values from -0.75 to 0.75
- w_o: bfloat16 [2048, 2048], P('tp'), may hold values from -0.125 to 0.125
Outputs:
- attention_out: bfloat16 [512, 2048], P('dp', 'tp')
Inputs may be any that keep to these rules, and one draw needn't show every extreme that they name: `lengths`: at least one live token in every request; some request reaches the most in every draw. For every request lend_counts[r, 0] + lend_counts[r, 1] is below its page count, so its first page is held by its own replica; every replica has a request that lends 2 pages each way. `page_table`: the 8 entries of a row are distinct. Entries for pages past a request's page count are not read.
All inputs are finite; a program needn't handle non-finite values.
Results may differ from a plain program's by a relative error of at most 0.012.
Values may be sent and summed in bfloat16 or wider, within the bound.
No kernel may reach another device: no remote copies, remote signals or barrier semaphores. Data moves between devices by JAX's collectives and lax.ppermute only.
A program may use at most 128 MiB of HBM per device.

v0:
```python
import functools
import math

import jax
import jax.numpy as jnp
from jax import lax
from jax.experimental import pallas as pl
from jax.experimental.pallas import tpu as pltpu
from jax.sharding import PartitionSpec as P

LEND = 2
LANES = 128
FIELDS = 16
ROW, LIVE, COUNT, SCORE_ROW = 2, 3, 4, 5
TABLE_ROWS = 6
FAR = -1e30
UNROLL = 8
PAIR = 2
MIB = 1 << 20


def swap(block, axis, odd_first):
    count = lax.axis_size(axis)
    shift = 1 if odd_first else 0
    pairs = []
    for start in range(shift, count + shift, 2):
        a, b = start % count, (start + 1) % count
        pairs += [(a, b), (b, a)]
    return lax.ppermute(block, axis, pairs)


def lane_tile(ref, index):
    return ref[:, index * LANES : (index + 1) * LANES]


def compact(fields, live_row, segment, spacing):
    height, lanes = fields.shape
    row = lax.broadcasted_iota(jnp.int32, (lanes, lanes), 0)
    column = lax.broadcasted_iota(jnp.int32, (lanes, lanes), 1)
    kept = jnp.where(fields[live_row : live_row + 1, :] > 0.0, 1.0, 0.0)
    kept = jnp.broadcast_to(kept, (height, lanes))
    ahead = (row // segment == column // segment) & (row < column)
    inside = row // segment == column // spacing
    place = jnp.dot(
        kept.astype(jnp.bfloat16),
        jnp.where(ahead, 1.0, 0.0).astype(jnp.bfloat16),
        preferred_element_type=jnp.float32,
    )
    count = jnp.dot(
        kept.astype(jnp.bfloat16),
        jnp.where(inside, 1.0, 0.0).astype(jnp.bfloat16),
        preferred_element_type=jnp.float32,
    )
    lane = lax.broadcasted_iota(jnp.int32, (height, lanes), 1)
    target = place.astype(jnp.int32) + lane // segment * spacing
    target = jnp.where(kept > 0.0, target, -1)
    chosen = jnp.where(jnp.broadcast_to(target[0:1, :], (lanes, lanes)) == row, 1.0, 0.0)
    moved = lax.dot_general(
        fields.astype(jnp.bfloat16),
        chosen.astype(jnp.bfloat16),
        (((1,), (1,)), ((), ())),
        preferred_element_type=jnp.float32,
    )
    return moved, count


def pack_kernel(lengths, table, lend, q_nope, q_rope, message, own, fields, *, page):
    rows = q_nope.shape[0]
    most = table.shape[0]
    shift = page.bit_length() - 1
    wide, narrow = q_nope.shape[1], q_rope.shape[1]
    length = lengths[...]
    count = lax.shift_right_logical(length + (page - 1), shift)
    to_prev, to_next = lend[0:1, :], lend[1:2, :]
    held = count - to_prev - to_next
    request = lax.broadcasted_iota(jnp.int32, (1, rows), 1)

    def pick(index):
        found = jnp.zeros_like(index)
        for k in range(most):
            found = jnp.where(index == k, table[k : k + 1, :], found)
        return found

    def lent(first, number):
        slots = [pick(jnp.minimum(first + k, count - 1)) for k in range(LEND)]
        live = jnp.minimum(length - first * page, number * page)
        return [*slots, request + 1, jnp.maximum(live, 0)]

    def stack(values, height):
        row = lax.broadcasted_iota(jnp.int32, (height, rows), 0)
        block = jnp.zeros((height, rows), jnp.int32)
        for k, value in enumerate(values):
            block = jnp.where(row == k, jnp.broadcast_to(value, (height, rows)), block)
        return block

    prev, nxt = lent(held, to_prev), lent(count - to_next, to_next)
    odd = lax.rem(lax.axis_index("dp"), 2) == 1
    fields[...] = jnp.zeros_like(fields)
    for k, (yes, no) in enumerate(((prev, nxt), (nxt, prev))):
        mine = stack([jnp.where(odd, p, n) for p, n in zip(yes, no)], FIELDS)
        fields[:, k * rows : (k + 1) * rows] = mine.astype(jnp.float32)
    moved, counts = compact(fields[...], LIVE, rows, LANES // 2)
    row = lax.broadcasted_iota(jnp.int32, (FIELDS, LANES), 0)
    asked = jnp.where(row == COUNT, counts, moved).astype(message.dtype)
    message[:, :wide] = q_nope[...]
    message[:, wide : wide + narrow] = q_rope[...]
    message[:, wide + narrow :] = jnp.concatenate(
        [asked, jnp.zeros((rows - FIELDS, LANES), message.dtype)], axis=0
    )
    own[...] = jnp.zeros_like(own)
    mine = [pick(jnp.minimum(k, held - 1)) for k in range(most)]
    own[:, :rows] = stack([*mine, jnp.minimum(length, held * page)], FIELDS)


def project_queries(message, w_uk, queries, heads, latent, narrow):
    rows = message.shape[0]
    nope = w_uk.shape[1]
    tiles = latent // LANES
    low = lax.broadcasted_iota(jnp.int32, (rows, LANES), 1) < LANES // 2
    for h in range(heads):
        lat = jnp.dot(
            message[:, h * nope : (h + 1) * nope], w_uk[h], preferred_element_type=jnp.float32
        )
        for c in range(tiles):
            queries[c, pl.ds(h, rows, stride=heads), :] = lat[:, c * LANES : (c + 1) * LANES]
    for c in range(narrow // LANES):
        pair = lane_tile(message, heads * nope // LANES + c).astype(jnp.float32)
        swapped = pltpu.roll(pair, LANES // 2, 1)
        for h, left, right in ((2 * c, pair, swapped), (2 * c + 1, swapped, pair)):
            at = pl.ds(h, rows, stride=heads)
            queries[tiles, at, :] = jnp.where(low, left, 0.0)
            queries[tiles + 1, at, :] = jnp.where(low, 0.0, right)


def to_table(moved, count, rows, heads, score_row=None):
    whole = moved.astype(jnp.int32)
    request = whole[ROW : ROW + 1, :]
    query_row = jnp.where(request == 0, rows, request - 1) * heads
    blocks = lax.shift_right_logical(
        count[0:1, :].astype(jnp.int32) + (UNROLL - 1), UNROLL.bit_length() - 1
    )
    row = lax.broadcasted_iota(jnp.int32, whole.shape, 0)
    for k, value in ((ROW, query_row), (COUNT, blocks)):
        whole = jnp.where(row == k, jnp.broadcast_to(value, whole.shape), whole)
    extra = query_row if score_row is None else query_row + score_row(whole)
    return jnp.where(row == SCORE_ROW, jnp.broadcast_to(extra, whole.shape), whole)


def rope_lanes(page, heads):
    quarter = page // 4
    lane = lax.broadcasted_iota(jnp.int32, (heads, LEND * page), 1)
    return lane // page * quarter + lax.rem(lane, page) // 4, lax.rem(lane, 4)


def latent_scores(queries, pool, items, heads):
    tiles = queries.shape[0] - 2
    left, rows = [], []
    for start, slots in items:
        at = pl.ds(start, heads)
        left.append(jnp.concatenate([queries[c, at, :] for c in range(tiles)], axis=1))
        rows += [pool[s] for s in slots]
    parts = lax.dot_general(
        jnp.concatenate(left, axis=0).astype(jnp.bfloat16),
        jnp.concatenate(rows, axis=0),
        (((1,), (1,)), ((), ())),
        preferred_element_type=jnp.float32,
    )
    columns = parts.shape[1] // len(items)
    for i in range(len(items)):
        yield parts[i * heads : (i + 1) * heads, i * columns : (i + 1) * columns]


def rope_scores(queries, rope_keys, items, lanes, heads):
    tiles = queries.shape[0] - 2
    left, rows = [], []
    for start, slots in items:
        turned = jnp.concatenate(
            [queries[tiles, pl.ds(start, heads), :], queries[tiles + 1, pl.ds(start, heads), :]],
            axis=0,
        ).astype(jnp.bfloat16)
        none = jnp.zeros_like(turned)
        left.append(jnp.concatenate([turned, none], axis=1))
        left.append(jnp.concatenate([none, turned], axis=1))
        rows += [rope_keys[s] for s in slots]
    parts = lax.dot_general(
        jnp.concatenate(left, axis=0),
        jnp.concatenate(rows, axis=0),
        (((1,), (1,)), ((), ())),
        preferred_element_type=jnp.float32,
    )
    source, which = lanes
    columns = parts.shape[1] // len(items)
    for i in range(len(items)):
        for j in range(4):
            first = (4 * i + j) * heads
            moved = jnp.take_along_axis(
                parts[first : first + heads, :], source + i * columns, axis=1
            )
            found = moved if j == 0 else jnp.where(which == j, moved, found)
        yield found


def fetch_rows(items, plan, sems):
    copies = [
        pltpu.make_async_copy(items.at[k], plan.at[pl.ds(k * LANES, LANES)], sems.at[k])
        for k in range(TABLE_ROWS)
    ]
    for copy in copies:
        copy.start()
    return copies


def read(plan, row, at):
    return plan[row * LANES + at]


def item(plan, at, heads):
    slots = [read(plan, k, at) for k in range(LEND)]
    return pl.multiple_of(read(plan, ROW, at), heads), slots


def score_work(queries, pool, rope_keys, scores, plan, base, heads, scale):
    page = pool.shape[1]
    scores[...] = jnp.full_like(scores, FAR)
    position = lax.broadcasted_iota(jnp.int32, (heads, LEND * page), 1)
    lanes = rope_lanes(page, heads)
    together = LANES // (LEND * (page // 4))

    @pl.loop(0, read(plan, COUNT, base))
    def _(block):
        first_item = base + block * UNROLL
        items = [item(plan, first_item + u, heads) for u in range(UNROLL)]
        ropes = []
        for first in range(0, UNROLL, together):
            ropes += rope_scores(queries, rope_keys, items[first : first + together], lanes, heads)
        for first in range(0, UNROLL, PAIR):
            mains = latent_scores(queries, pool, items[first : first + PAIR], heads)
            for u, main in enumerate(mains, first):
                start = pl.multiple_of(read(plan, SCORE_ROW, first_item + u), heads)
                scores[pl.ds(start, heads), :] = jnp.where(
                    position < read(plan, LIVE, first_item + u), (main + ropes[u]) * scale, FAR
                )


def soften(scores, weights, norm, lse, total_rows):
    pitch = total_rows + (scores.shape[0] % total_rows) // (scores.shape[0] // total_rows)
    units = scores.shape[0] // pitch
    step = 64
    for r in range(0, total_rows, step):
        block = [scores[j * pitch + r : j * pitch + r + step, :] for j in range(units)]
        top = block[0]
        for one in block[1:]:
            top = jnp.maximum(top, one)
        peak = jnp.max(top, axis=-1, keepdims=True)
        total = jnp.zeros((step, LANES), jnp.float32)
        for j in range(units):
            rounded = jnp.exp(block[j] - peak).astype(jnp.bfloat16).astype(jnp.float32)
            weights[j * pitch + r : j * pitch + r + step, :] = rounded
            total = total + rounded
        total = jnp.sum(total, axis=-1, keepdims=True)
        norm[r : r + step, :] = jnp.broadcast_to(1.0 / total, (step, LANES))
        lse[r : r + step, :] = jnp.broadcast_to(peak + jnp.log(total), (step, LANES))


def value_work(pool, weights, context, plan, base, heads, add):
    @pl.loop(0, read(plan, COUNT, base))
    def _(block):
        for first in range(0, UNROLL, PAIR):
            starts, left, values = [], [], []
            for u in range(first, first + PAIR):
                at = base + block * UNROLL + u
                start, slots = item(plan, at, heads)
                starts.append(start)
                mine = weights[pl.ds(pl.multiple_of(read(plan, SCORE_ROW, at), heads), heads), :]
                none = jnp.zeros_like(mine)
                left.append(
                    jnp.concatenate(
                        [mine if k == u - first else none for k in range(PAIR)], axis=1
                    )
                )
                values += [pool[s] for s in slots]
            summed = jnp.dot(
                jnp.concatenate(left, axis=0).astype(jnp.bfloat16),
                jnp.concatenate(values, axis=0),
                preferred_element_type=jnp.float32,
            )
            for k, start in enumerate(starts):
                for c in range(context.shape[0]):
                    part = summed[k * heads : (k + 1) * heads, c * LANES : (c + 1) * LANES]
                    if add:
                        part = part + context[c, pl.ds(start, heads), :]
                    context[c, pl.ds(start, heads), :] = part


def head_outs(context, norm, w_uv, rows, heads):
    width = w_uv.shape[2]
    for h in range(0, heads, 2):
        pair = []
        for k in range(2):
            at = pl.ds(h + k, rows, stride=heads)
            scale = norm[at, :]
            pair.append(
                jnp.concatenate([context[c, at, :] * scale for c in range(context.shape[0])], axis=1)
            )
        both = jnp.dot(
            jnp.concatenate(pair, axis=0).astype(jnp.bfloat16),
            jnp.concatenate([w_uv[h], w_uv[h + 1]], axis=1),
            preferred_element_type=jnp.float32,
        )
        yield h, both[:rows, :width]
        yield h + 1, both[rows:, width:]


def own_scores_kernel(
    own, message, rope_hbm, pool_hbm, w_uk_hbm,
    pool, rope_keys, weights, norm, lse, items,
    queries, scores, spread, rope_pages, w_uk, fields, plan, sems, plan_sem,
    *, heads, narrow, most,
):
    slots, page, latent = pool.shape
    rows = message.shape[0]
    units = most // LEND
    scale = 1.0 / math.sqrt(w_uk.shape[1] + narrow // heads)
    routes = ((rope_hbm, rope_pages), (w_uk_hbm, w_uk), (pool_hbm, pool))
    fetches = [pltpu.make_async_copy(*route, sems.at[k]) for k, route in enumerate(routes)]
    for fetch in fetches:
        fetch.start()
    tokens = LEND * page
    fields[...] = jnp.zeros_like(fields)
    request = lax.broadcasted_iota(jnp.int32, (1, rows), 1)
    for j in range(units):
        live = jnp.clip(own[most : most + 1, :rows] - j * tokens, 0, tokens)
        values = [own[j * LEND + k : j * LEND + k + 1, :rows] for k in range(LEND)]
        values += [request + 1, live, jnp.zeros_like(live), jnp.full_like(live, j)]
        for k, value in enumerate(values):
            fields[k : k + 1, j * rows : (j + 1) * rows] = value.astype(jnp.float32)
    moved, count = compact(fields[...], LIVE, LANES, LANES)
    pitch = (rows + 1) * heads
    items[...] = to_table(moved, count, rows, heads, lambda w: w[SCORE_ROW : SCORE_ROW + 1, :] * pitch)
    table = fetch_rows(items, plan, plan_sem)
    fetches[0].wait()
    pieces = page // 2
    spacing = pieces + 1
    for c in range(pieces):
        spread[pl.ds(c, slots, stride=spacing), :] = lane_tile(rope_pages, c).astype(jnp.float32)
    for s in range(slots):
        for side in range(2):
            rows_of = spread[pl.ds(s * spacing + side, pieces // 2, stride=2), :]
            rope_keys[s, :, side * LANES : (side + 1) * LANES] = rows_of.astype(jnp.bfloat16)
    fetches[1].wait()
    project_queries(message, w_uk, queries, heads, latent, narrow)
    for copy in table:
        copy.wait()
    fetches[2].wait()
    score_work(queries, pool, rope_keys, scores, plan, 0, heads, scale)
    soften(scores, weights, norm, lse, rows * heads)


def own_values_kernel(items, pool, weights, norm, w_uv, outs, context, plan, plan_sem, *, heads):
    rows = outs.shape[0]
    table = fetch_rows(items, plan, plan_sem)
    context[...] = jnp.zeros_like(context)
    for copy in table:
        copy.wait()
    value_work(pool, weights, context, plan, 0, heads, True)
    width = w_uv.shape[2]
    for h, out in head_outs(context, norm, w_uv, rows, heads):
        outs[:, h * width : (h + 1) * width] = out


def serve_kernel(
    message, pool, rope_keys, w_uk, w_uv, back,
    queries, scores, weights, norm, lse, context, items, plan, plan_sem,
    *, narrow, base,
):
    rows = message.shape[0]
    slots, page, latent = pool.shape
    heads = w_uk.shape[0]
    scale = 1.0 / math.sqrt(w_uk.shape[1] + narrow // heads)
    asked = message[0:FIELDS, message.shape[1] - LANES :].astype(jnp.float32)
    items[...] = to_table(asked, asked[COUNT : COUNT + 1, :], rows, heads)
    table = fetch_rows(items, plan, plan_sem)
    context[...] = jnp.zeros_like(context)
    project_queries(message, w_uk, queries, heads, latent, narrow)
    for copy in table:
        copy.wait()
    score_work(queries, pool, rope_keys, scores, plan, base, heads, scale)
    soften(scores, weights, norm, lse, rows * heads)
    value_work(pool, weights, context, plan, base, heads, False)
    width = w_uv.shape[2]
    lane = lax.broadcasted_iota(jnp.int32, (rows, LANES), 1)
    logs = jnp.zeros((rows, LANES), jnp.float32)
    for h, out in head_outs(context, norm, w_uv, rows, heads):
        back[:, h * width : (h + 1) * width] = out.astype(jnp.bfloat16)
        logs = jnp.where(lax.rem(lane, heads) == h, lse[pl.ds(h, rows, stride=heads), :], logs)
    packed = jnp.zeros((rows, LANES), jnp.float32)
    for part in range(3):
        piece = logs.astype(jnp.bfloat16).astype(jnp.float32)
        logs = logs - piece
        packed = jnp.where(lane // heads == part, piece, packed)
    back[:, heads * width :] = packed.astype(jnp.bfloat16)


def join_kernel(outs, lse, from_a, from_b, w_o, sent, kept, joined, *, heads):
    rows = outs.shape[0]
    width = outs.shape[1] // heads
    totals = []
    for arrived in (from_a, from_b):
        tile = arrived[:, heads * width :].astype(jnp.float32)
        total = tile + pltpu.roll(tile, LANES - heads, 1) + pltpu.roll(tile, LANES - 2 * heads, 1)
        totals.append(total)
    for h in range(heads):
        at = slice(h * width, (h + 1) * width)
        logs = [lse[pl.ds(h, rows, stride=heads), :]]
        values = [outs[:, at]]
        for arrived, total in zip((from_a, from_b), totals):
            logs.append(jnp.broadcast_to(total[:, h : h + 1], (rows, LANES)))
            values.append(arrived[:, at].astype(jnp.float32))
        peak = jnp.maximum(jnp.maximum(logs[0], logs[1]), logs[2])
        shares = [jnp.exp(one - peak) for one in logs]
        top = shares[0] * values[0] + shares[1] * values[1] + shares[2] * values[2]
        joined[:, at] = (top / (shares[0] + shares[1] + shares[2])).astype(jnp.bfloat16)
    mine = lax.axis_index("tp")
    other = lax.rem(mine + 1, lax.axis_size("tp"))
    cols = sent.shape[1]
    heads_joined = joined[...]
    away = pl.ds(pl.multiple_of(other * cols, cols), cols)
    here = pl.ds(pl.multiple_of(mine * cols, cols), cols)
    sent[...] = jnp.dot(
        heads_joined, w_o[:, away], preferred_element_type=jnp.float32
    ).astype(jnp.bfloat16)
    kept[...] = jnp.dot(heads_joined, w_o[:, here], preferred_element_type=jnp.float32)


def vmem():
    return pl.BlockSpec(memory_space=pltpu.VMEM)


def in_hbm(array):
    return pltpu.with_memory_space_constraint(array, pltpu.HBM)


def call(kernel, name, out, ins, scratch, limit, cost=None, **sizes):
    return pl.pallas_call(
        functools.partial(kernel, **sizes),
        name=name,
        out_shape=out,
        in_specs=ins,
        out_specs=jax.tree.map(lambda _: vmem(), out),
        scratch_shapes=scratch,
        compiler_params=pltpu.CompilerParams(vmem_limit_bytes=limit * MIB),
        cost_estimate=cost,
    )


def shards(
    q_nope, q_rope, lengths, page_table, lend_counts, latent_pages, rope_pages, w_uk, w_uv, w_o
):
    rows = lengths.shape[0]
    heads, nope, latent = w_uk.shape
    slots, page, _ = latent_pages.shape
    most = page_table.shape[1]
    width = w_uv.shape[2]
    narrow = q_rope.shape[1]
    tiles = latent // LANES
    units = most // LEND
    assert rows * units <= LANES and FIELDS <= rows <= LANES // 2 and page * LEND == LANES
    f32, bf16, i32 = jnp.float32, jnp.bfloat16, jnp.int32
    shape = jax.ShapeDtypeStruct
    sem = pltpu.SemaphoreType.DMA
    stats = (rows * heads, LANES)
    padded = (rows + 1) * heads
    block = pltpu.VMEM((tiles + 2, padded, LANES), f32)
    contexts = pltpu.VMEM((tiles, padded, LANES), f32)
    plan = pltpu.SMEM((TABLE_ROWS * LANES,), i32)

    message, own = call(
        pack_kernel,
        "pack",
        (shape((rows, heads * nope + narrow + LANES), bf16), shape((FIELDS, LANES), i32)),
        [vmem()] * 5,
        [pltpu.VMEM((FIELDS, LANES), f32)],
        4,
        page=page,
    )(*map(in_hbm, (lengths.reshape(1, rows), page_table.T, lend_counts.T, q_nope, q_rope)))
    asked_a = swap(message, "dp", False)
    asked_b = swap(message, "dp", True)

    pool, rope_keys, weights, norm, lse, items = call(
        own_scores_kernel,
        "own_scores",
        (
            shape((slots, page, latent), bf16),
            shape((slots, page // 4, 2 * LANES), bf16),
            shape((units * padded, LANES), f32),
            shape(stats, f32),
            shape(stats, f32),
            shape((FIELDS, LANES), i32),
        ),
        [vmem()] * 2 + [pl.BlockSpec(memory_space=pl.ANY)] * 3,
        [
            block,
            pltpu.VMEM((units * padded, LANES), f32),
            pltpu.VMEM((slots * (page // 2 + 1), LANES), f32),
            pltpu.VMEM(rope_pages.shape, bf16),
            pltpu.VMEM(w_uk.shape, bf16),
            pltpu.VMEM((FIELDS, LANES), f32),
            plan,
            sem((3,)),
            sem((TABLE_ROWS,)),
        ],
        24,
        pl.CostEstimate(
            flops=2 * rows * heads * most * page * (latent + LANES),
            bytes_accessed=slots * page * (latent + LANES) * 2,
            transcendentals=rows * heads * most * page,
        ),
        heads=heads,
        narrow=narrow,
        most=most,
    )(own, message, *map(in_hbm, (rope_pages, latent_pages, w_uk)))

    serve_scratch = [
        block,
        pltpu.VMEM((padded, LANES), f32),
        pltpu.VMEM((padded, LANES), f32),
        pltpu.VMEM(stats, f32),
        pltpu.VMEM(stats, f32),
        contexts,
        pltpu.VMEM((FIELDS, LANES), i32),
        plan,
        sem((TABLE_ROWS,)),
    ]

    def serve(asked, name, base):
        return call(
            serve_kernel,
            name,
            shape((rows, heads * width + LANES), bf16),
            [vmem()] * 5,
            serve_scratch,
            8,
            narrow=narrow,
            base=base,
        )(asked, pool, rope_keys, w_uk, w_uv)

    from_b = swap(serve(asked_b, "serve_b", LANES // 2), "dp", True)
    from_a = swap(serve(asked_a, "serve_a", 0), "dp", False)
    outs = call(
        own_values_kernel,
        "own_values",
        shape((rows, heads * width), f32),
        [vmem()] * 5,
        [contexts, plan, sem((TABLE_ROWS,))],
        8,
        heads=heads,
    )(items, pool, weights, norm, w_uv)
    cols = w_o.shape[1] // lax.axis_size("tp")
    sent, kept = call(
        join_kernel,
        "join",
        (shape((rows, cols), bf16), shape((rows, cols), f32)),
        [vmem()] * 5,
        [pltpu.VMEM((rows, heads * width), bf16)],
        8,
        heads=heads,
    )(outs, lse, from_a, from_b, w_o)
    return (kept + swap(sent, "tp", False).astype(f32)).astype(bf16)


def solution(mesh):
    in_specs = (
        P("dp", "tp"),
        P("dp", "tp"),
        P("dp"),
        P("dp", None),
        P("dp", None),
        P("dp", None, None),
        P("dp", None),
        P("tp", None, None),
        P("tp", None, None),
        P("tp", None),
    )
    out_specs = P("dp", "tp")
    return jax.shard_map(shards, mesh=mesh, in_specs=in_specs, out_specs=out_specs, check_vma=False)
```

profile of v0, /device:TPU:0, one launch (start us, length us, event | category | flops | bytes accessed | tf_op | source)
XLA Modules:
  0.0 29.5 jit_solution(7481550057360875976)
XLA Ops:
  0.0 0.0 copy-start.1
  0.0 0.0 copy-start
  0.0 1.4 %pack.1 = (bf16[32,1664]{1,0:T(8,128)(2,1)S(1)}, s32[16,128]{1,0:T(8,128)S(1)}) custom-call(s32[1,32]{1,0:T(1,128)} %bitcast.5, s32[8,32]{1,0:T(8,128)} %bitcast.3, s32[2,32]{1,0:T(2,128)} %bitcast.4, bf16[32,1024]{1,0:T(8,128)(2,1)} %q_nope.1, bf16[32,512]{1,0:T(8,128)(2,1)} %q_rope.1), custom_call_target="tpu_custom_call" | custom-call | tf_op jit(solution)/shard_map/pack/pallas_call | solution.py:477
  1.4 5.4 %collective-permute-start.2 = (bf16[32,1664]{1,0:T(8,128)(2,1)S(1)}, bf16[32,1664]{1,0:T(8,128)(2,1)S(1)}, u32[]{:S(2)}, u32[]{:S(2)}) collective-permute-start(bf16[32,1664]{1,0:T(8,128)(2,1)S(1)} %get-tuple-element.16.message), channel_id=1, source_target_pairs={{2,4},{4,2},{6,8},{8,6},{10,12},{12,10},{14,16},{16,14},{18,20},{2... | collective-permute-start | bytes 319496 | tf_op jit(solution)/shard_map/ppermute | solution.py:29
  6.8 0.0 collective-permute-start
  6.8 6.0 %own_scores.1 = (bf16[96,64,512]{2,1,0:T(8,128)(2,1)S(1)}, bf16[96,16,256]{2,1,0:T(8,128)(2,1)S(1)}, f32[1056,128]{1,0:T(8,128)S(1)}, f32[256,128]{1,0:T(8,128)S...) custom-call(s32[16,128]{1,0:T(8,128)S(1)} %get-tuple-element.15.own, bf16[32,1664]{1,0:T(8,128)(2,1)S(1)} %get-tuple-element.16.message, ...), custom_call_target="tpu_custom_call" | custom-call | flops 167772160 | bytes 7864320 | tf_op jit(solution)/shard_map/own_scores/pallas_call | solution.py:489
  12.8 0.0 collective-permute-done.2.message
  12.8 0.0 copy-done.1
  12.8 0.0 copy-done
  12.8 4.2 %serve_b.1 = bf16[32,1152]{1,0:T(8,128)(2,1)S(1)} custom-call(bf16[32,1664]{1,0:T(8,128)(2,1)S(1)} %collective-permute-done.2.message, bf16[96,64,512]{2,1,0:T(8,128)(2,1)S(1)} %get-tuple-element.18.pool, bf16[96,16,256]{2,1,0:T(8,128)(2,1)S(1)} %get-tuple-element.22.rope_keys, bf16[8,128,512]{2,1,0:T(8,128)(2,1)S(1)} %copy-done.1, ...), custom_call_target="tpu_custom_call" | custom-call | tf_op jit(solution)/shard_map/serve_b/pallas_call | solution.py:536
  17.0 0.5 %collective-permute-start.3 = (bf16[32,1152]{1,0:T(8,128)(2,1)S(1)}, bf16[32,1152]{1,0:T(8,128)(2,1)S(1)}, u32[]{:S(2)}, u32[]{:S(2)}) collective-permute-start(bf16[32,1152]{1,0:T(8,128)(2,1)S(1)} %serve_b.1), channel_id=1, source_target_pairs={{2,4},{4,2},{6,8},{8,6},{10,12},{12,10},{14,16},{16,14},{18,20},{2... | collective-permute-start | bytes 221192 | tf_op jit(solution)/shard_map/ppermute | solution.py:29
  17.5 0.0 collective-permute-done.message
  17.5 2.1 %serve_a.1 = bf16[32,1152]{1,0:T(8,128)(2,1)S(1)} custom-call(bf16[32,1664]{1,0:T(8,128)(2,1)S(1)} %collective-permute-done.message, bf16[96,64,512]{2,1,0:T(8,128)(2,1)S(1)} %get-tuple-element.18.pool, bf16[96,16,256]{2,1,0:T(8,128)(2,1)S(1)} %get-tuple-element.22.rope_keys, bf16[8,128,512]{2,1,0:T(8,128)(2,1)S(1)} %copy-done.1, ...), custom_call_target="tpu_custom_call" | custom-call | tf_op jit(solution)/shard_map/serve_a/pallas_call | solution.py:536
  19.6 0.0 copy-start.2
  19.6 0.1 collective-permute-start.1
  19.6 2.2 %own_values.1.outs = f32[32,1024]{1,0:T(8,128)S(1)} custom-call(s32[16,128]{1,0:T(8,128)S(1)} %get-tuple-element.17.items, bf16[96,64,512]{2,1,0:T(8,128)(2,1)S(1)} %get-tuple-element.18.pool, f32[1056,128]{1,0:T(8,128)S(1)} %get-tuple-element.19.weights, f32[256,128]{1,0:T(8,128)S(1)} %get-tuple-element.20.norm, bf16[8,512,128]{2,1,0:T(8,128)(2,1)S(1)} %copy-done), custom_call_target="tpu_custom_call" | custom-call | tf_op jit(solution)/shard_map/own_values/pallas_call | solution.py:549
  21.8 1.7 %collective-permute-done.3.from_b = bf16[32,1152]{1,0:T(8,128)(2,1)S(1)} collective-permute-done((bf16[32,1152]{1,0:T(8,128)(2,1)S(1)}, bf16[32,1152]{1,0:T(8,128)(2,1)S(1)}, u32[]{:S(2)}, u32[]{:S(2)}) %collective-permute-start.3) | collective-permute-done | bytes 73760 | tf_op jit(solution)/shard_map/ppermute | solution.py:29
  23.5 0.0 collective-permute-done.1.from_a
  23.6 0.0 copy-done.2
  23.6 1.0 %join.1 = (bf16[32,1024]{1,0:T(8,128)(2,1)S(1)}, f32[32,1024]{1,0:T(8,128)S(1)}) custom-call(f32[32,1024]{1,0:T(8,128)S(1)} %own_values.1.outs, f32[256,128]{1,0:T(8,128)S(1)} %get-tuple-element.21.lse, bf16[32,1152]{1,0:T(8,128)(2,1)S(1)} %collective-permute-done.1.from_a, bf16[32,1152]{1,0:T(8,128)(2,1)S(1)} %collective-permute-done.3.from_b, ...), custom_call_target="tpu_custom_call" | custom-call | tf_op jit(solution)/shard_map/join/pallas_call | solution.py:559
  24.5 1.5 %collective-permute-start.4 = (bf16[32,1024]{1,0:T(8,128)(2,1)S(1)}, bf16[32,1024]{1,0:T(8,128)(2,1)S(1)}, u32[]{:S(2)}, u32[]{:S(2)}) collective-permute-start(bf16[32,1024]{1,0:T(8,128)(2,1)S(1)} %get-tuple-element.24), channel_id=1, source_target_pairs={{0,1},{1,0},{2,3},{3,2},{4,5},{5,4},{6,7},{7,6},{8,9},{9,8},{10,11... | collective-permute-start | bytes 196616 | tf_op jit(solution)/shard_map/ppermute | solution.py:29
  26.1 2.7 %collective-permute-done.4 = bf16[32,1024]{1,0:T(8,128)(2,1)S(1)} collective-permute-done((bf16[32,1024]{1,0:T(8,128)(2,1)S(1)}, bf16[32,1024]{1,0:T(8,128)(2,1)S(1)}, u32[]{:S(2)}, u32[]{:S(2)}) %collective-permute-start.4) | collective-permute-done | bytes 65568 | tf_op jit(solution)/shard_map/ppermute | solution.py:29
  28.8 0.6 %add_convert_fusion = bf16[32,1024]{1,0:T(8,128)(2,1)} fusion(f32[32,1024]{1,0:T(8,128)S(1)} %get-tuple-element.23, bf16[32,1024]{1,0:T(8,128)(2,1)S(1)} %collective-permute-done.4), kind=kLoop, calls=%fused_computation | loop fusion | flops 98304 | bytes 262144 | tf_op jit(solution)/shard_map/convert_element_type | solution.py:568
Async XLA Ops:
  0.0 12.8 %copy-start.1 = (bf16[8,128,512]{2,1,0:T(8,128)(2,1)S(1)}, bf16[8,128,512]{2,1,0:T(8,128)(2,1)}, u32[]{:S(2)}) copy-start(bf16[8,128,512]{2,1,0:T(8,128)(2,1)} %w_uk.3) | copy-start | bytes 3145732
  0.0 12.8 %copy-start = (bf16[8,512,128]{2,1,0:T(8,128)(2,1)S(1)}, bf16[8,512,128]{2,1,0:T(8,128)(2,1)}, u32[]{:S(2)}) copy-start(bf16[8,512,128]{2,1,0:T(8,128)(2,1)} %w_uv.5) | copy-start | bytes 3145732
  1.4 11.4 %collective-permute-start.2 = (bf16[32,1664]{1,0:T(8,128)(2,1)S(1)}, bf16[32,1664]{1,0:T(8,128)(2,1)S(1)}, u32[]{:S(2)}, u32[]{:S(2)}) collective-permute-start(bf16[32,1664]{1,0:T(8,128)(2,1)S(1)} %get-tuple-element.16.message), channel_id=1, source_target_pairs={{2,4},{4,2},{6,8},{8,6},{10,12},{12,10},{14,16},{16,14},{18,20},{2... | collective-permute-start | bytes 319496 | tf_op jit(solution)/shard_map/ppermute | solution.py:29
  6.8 10.7 %collective-permute-start = (bf16[32,1664]{1,0:T(8,128)(2,1)S(1)}, bf16[32,1664]{1,0:T(8,128)(2,1)S(1)}, u32[]{:S(2)}, u32[]{:S(2)}) collective-permute-start(bf16[32,1664]{1,0:T(8,128)(2,1)S(1)} %get-tuple-element.16.message), channel_id=1, source_target_pairs={{0,2},{2,0},{4,6},{6,4},{8,10},{10,8},{12,14},{14,12},{16,18},{18,... | collective-permute-start | bytes 319496 | tf_op jit(solution)/shard_map/ppermute | solution.py:29
  17.0 6.5 %collective-permute-start.3 = (bf16[32,1152]{1,0:T(8,128)(2,1)S(1)}, bf16[32,1152]{1,0:T(8,128)(2,1)S(1)}, u32[]{:S(2)}, u32[]{:S(2)}) collective-permute-start(bf16[32,1152]{1,0:T(8,128)(2,1)S(1)} %serve_b.1), channel_id=1, source_target_pairs={{2,4},{4,2},{6,8},{8,6},{10,12},{12,10},{14,16},{16,14},{18,20},{2... | collective-permute-start | bytes 221192 | tf_op jit(solution)/shard_map/ppermute | solution.py:29
  19.6 4.0 %copy-start.2 = (bf16[1024,2048]{1,0:T(8,128)(2,1)S(1)}, bf16[1024,2048]{1,0:T(8,128)(2,1)}, u32[]{:S(2)}) copy-start(bf16[1024,2048]{1,0:T(8,128)(2,1)} %w_o.1) | copy-start | bytes 12582916
  19.6 4.0 %collective-permute-start.1 = (bf16[32,1152]{1,0:T(8,128)(2,1)S(1)}, bf16[32,1152]{1,0:T(8,128)(2,1)S(1)}, u32[]{:S(2)}, u32[]{:S(2)}) collective-permute-start(bf16[32,1152]{1,0:T(8,128)(2,1)S(1)} %serve_a.1), channel_id=1, source_target_pairs={{0,2},{2,0},{4,6},{6,4},{8,10},{10,8},{12,14},{14,12},{16,18},{18,... | collective-permute-start | bytes 221192 | tf_op jit(solution)/shard_map/ppermute | solution.py:29
  24.5 4.3 %collective-permute-start.4 = (bf16[32,1024]{1,0:T(8,128)(2,1)S(1)}, bf16[32,1024]{1,0:T(8,128)(2,1)S(1)}, u32[]{:S(2)}, u32[]{:S(2)}) collective-permute-start(bf16[32,1024]{1,0:T(8,128)(2,1)S(1)} %get-tuple-element.24), channel_id=1, source_target_pairs={{0,1},{1,0},{2,3},{3,2},{4,5},{5,4},{6,7},{7,6},{8,9},{9,8},{10,11... | collective-permute-start | bytes 196616 | tf_op jit(solution)/shard_map/ppermute | solution.py:29
where the time goes:
time: 29.6 us; the launch traced here: 29.5 us
  Pallas kernels  16.8 us (57%)
  starting transfers between devices  7.52 us (25%)
  waiting for transfers between devices  4.45 us (15%)
  other arithmetic  0.65 us (2%)
    ppermute x5, starting transfers between devices, swap(): return lax.ppermute(block, axis, pairs)  7.52 us
    pallas_call x2, Pallas kernels, serve(): call(serve_kernel, name, shape((rows, heads * width + LANES), bf16), [vme...  6.22 us
    pallas_call x1, Pallas kernels, shards(): call(own_scores_kernel, 'own_scores', (shape((slots, page, latent), bf16)...  5.97 us
    ppermute x5, waiting for transfers between devices, swap(): return lax.ppermute(block, axis, pairs)  4.45 us
    pallas_call x1, Pallas kernels, shards(): call(own_values_kernel, 'own_values', shape((rows, heads * width), f32),...  2.2 us
    pallas_call x1, Pallas kernels, shards(): call(pack_kernel, 'pack', (shape((rows, heads * nope + narrow + LANES), b...  1.38 us
    pallas_call x1, Pallas kernels, shards(): call(join_kernel, 'join', (shape((rows, cols), bf16), shape((rows, cols),...  0.99 us
    convert_element_type x1, other arithmetic, shards(): return (kept + swap(sent, 'tp', False).astype(f32)).astype(bf16)  0.65 us
  transfers between devices with their start and end apart: 5, of which 2 were waited for; matrix products, arithmetic and copies ran while one was open for 0% of the time, Pallas kernels for 49%

commit v1 on v0

--- a/solution.py
+++ b/solution.py
@@ -7,6 +7,7 @@
 from jax.experimental import pallas as pl
 from jax.experimental.pallas import tpu as pltpu
 from jax.sharding import PartitionSpec as P
+
 
 LEND = 2
 LANES = 128
@@ -312,19 +313,15 @@
 
 
 def own_scores_kernel(
-    own, message, rope_hbm, pool_hbm, w_uk_hbm,
-    pool, rope_keys, weights, norm, lse, items,
-    queries, scores, spread, rope_pages, w_uk, fields, plan, sems, plan_sem,
+    own, message, rope_pages, pool, w_uk,
+    rope_keys, weights, norm, lse, items,
+    queries, scores, spread, fields, plan, plan_sem,
     *, heads, narrow, most,
 ):
     slots, page, latent = pool.shape
     rows = message.shape[0]
     units = most // LEND
     scale = 1.0 / math.sqrt(w_uk.shape[1] + narrow // heads)
-    routes = ((rope_hbm, rope_pages), (w_uk_hbm, w_uk), (pool_hbm, pool))
-    fetches = [pltpu.make_async_copy(*route, sems.at[k]) for k, route in enumerate(routes)]
-    for fetch in fetches:
-        fetch.start()
     tokens = LEND * page
     fields[...] = jnp.zeros_like(fields)
     request = lax.broadcasted_iota(jnp.int32, (1, rows), 1)
@@ -338,7 +335,6 @@
     pitch = (rows + 1) * heads
     items[...] = to_table(moved, count, rows, heads, lambda w: w[SCORE_ROW : SCORE_ROW + 1, :] * pitch)
     table = fetch_rows(items, plan, plan_sem)
-    fetches[0].wait()
     pieces = page // 2
     spacing = pieces + 1
     for c in range(pieces):
@@ -347,11 +343,9 @@
         for side in range(2):
             rows_of = spread[pl.ds(s * spacing + side, pieces // 2, stride=2), :]
             rope_keys[s, :, side * LANES : (side + 1) * LANES] = rows_of.astype(jnp.bfloat16)
-    fetches[1].wait()
     project_queries(message, w_uk, queries, heads, latent, narrow)
     for copy in table:
         copy.wait()
-    fetches[2].wait()
     score_work(queries, pool, rope_keys, scores, plan, 0, heads, scale)
     soften(scores, weights, norm, lse, rows * heads)
 
@@ -374,7 +368,7 @@
     *, narrow, base,
 ):
     rows = message.shape[0]
-    slots, page, latent = pool.shape
+    _, _, latent = pool.shape
     heads = w_uk.shape[0]
     scale = 1.0 / math.sqrt(w_uk.shape[1] + narrow // heads)
     asked = message[0:FIELDS, message.shape[1] - LANES :].astype(jnp.float32)
@@ -440,10 +434,9 @@
     return pltpu.with_memory_space_constraint(array, pltpu.HBM)
 
 
-def call(kernel, name, out, ins, scratch, limit, cost=None, **sizes):
+def call(kernel, out, ins, scratch, limit, cost=None, **sizes):
     return pl.pallas_call(
         functools.partial(kernel, **sizes),
-        name=name,
         out_shape=out,
         in_specs=ins,
         out_specs=jax.tree.map(lambda _: vmem(), out),
@@ -476,37 +469,32 @@
 
     message, own = call(
         pack_kernel,
-        "pack",
         (shape((rows, heads * nope + narrow + LANES), bf16), shape((FIELDS, LANES), i32)),
         [vmem()] * 5,
         [pltpu.VMEM((FIELDS, LANES), f32)],
         4,
+        pl.CostEstimate(flops=20 * 10**9, bytes_accessed=64 * MIB, transcendentals=10**7),
         page=page,
     )(*map(in_hbm, (lengths.reshape(1, rows), page_table.T, lend_counts.T, q_nope, q_rope)))
+    asked_b = swap(message, "dp", True)
     asked_a = swap(message, "dp", False)
-    asked_b = swap(message, "dp", True)
-
-    pool, rope_keys, weights, norm, lse, items = call(
+
+    rope_keys, weights, norm, lse, items = call(
         own_scores_kernel,
-        "own_scores",
         (
-            shape((slots, page, latent), bf16),
             shape((slots, page // 4, 2 * LANES), bf16),
             shape((units * padded, LANES), f32),
             shape(stats, f32),
             shape(stats, f32),
             shape((FIELDS, LANES), i32),
         ),
-        [vmem()] * 2 + [pl.BlockSpec(memory_space=pl.ANY)] * 3,
+        [vmem()] * 5,
         [
             block,
             pltpu.VMEM((units * padded, LANES), f32),
             pltpu.VMEM((slots * (page // 2 + 1), LANES), f32),
-            pltpu.VMEM(rope_pages.shape, bf16),
-            pltpu.VMEM(w_uk.shape, bf16),
             pltpu.VMEM((FIELDS, LANES), f32),
             plan,
-            sem((3,)),
             sem((TABLE_ROWS,)),
         ],
         24,
@@ -518,7 +506,7 @@
         heads=heads,
         narrow=narrow,
         most=most,
-    )(own, message, *map(in_hbm, (rope_pages, latent_pages, w_uk)))
+    )(own, message, rope_pages, latent_pages, w_uk)
 
     serve_scratch = [
         block,
@@ -532,33 +520,32 @@
         sem((TABLE_ROWS,)),
     ]
 
-    def serve(asked, name, base):
+    def serve(asked, base):
         return call(
             serve_kernel,
-            name,
             shape((rows, heads * width + LANES), bf16),
             [vmem()] * 5,
             serve_scratch,
             8,
             narrow=narrow,
             base=base,
-        )(asked, pool, rope_keys, w_uk, w_uv)
-
-    from_b = swap(serve(asked_b, "serve_b", LANES // 2), "dp", True)
-    from_a = swap(serve(asked_a, "serve_a", 0), "dp", False)
+        )(asked, latent_pages, rope_keys, w_uk, w_uv)
+
+    back_b = serve(asked_b, LANES // 2)
+    from_b = swap(back_b, "dp", True)
+    back_a = serve(asked_a, 0)
+    from_a = swap(back_a, "dp", False)
     outs = call(
         own_values_kernel,
-        "own_values",
         shape((rows, heads * width), f32),
         [vmem()] * 5,
         [contexts, plan, sem((TABLE_ROWS,))],
         8,
         heads=heads,
-    )(items, pool, weights, norm, w_uv)
+    )(items, latent_pages, weights, norm, w_uv)
     cols = w_o.shape[1] // lax.axis_size("tp")
     sent, kept = call(
         join_kernel,
-        "join",
         (shape((rows, cols), bf16), shape((rows, cols), f32)),
         [vmem()] * 5,
         [pltpu.VMEM((rows, heads * width), bf16)],
@@ -582,4 +569,5 @@
         P("tp", None),
     )
     out_specs = P("dp", "tp")
+
     return jax.shard_map(shards, mesh=mesh, in_specs=in_specs, out_specs=out_specs, check_vma=False)

time: 29.6 us -> 28.7 us (0.970)
  Pallas kernels: 16.8 us -> 13 us
  starting transfers between devices: 7.52 us -> 9.06 us
  waiting for transfers between devices: 4.45 us -> 5.74 us
    pallas_call x6, Pallas kernels: 16.8 us -> 13 us  [the longest x2 4.82 us: serve(): call(serve_kernel, shape((rows, heads * width + LANES), bf16), [vmem()] *...]
    ppermute x5, starting transfers between devices: 7.52 us -> 9.06 us  [swap(): return lax.ppermute(block, axis, pairs)]
    ppermute x5, waiting for transfers between devices: 4.45 us -> 5.74 us  [swap(): return lax.ppermute(block, axis, pairs)]
  transfers between devices with their start and end apart: 5 -> 5, of which waited for: 2 -> 2; matrix products, arithmetic and copies ran while one was open for 0% -> 0% of each run, Pallas kernels for 49% -> 37%
where the time goes in v1:
time: 28.7 us; the launch traced here: 28.6 us
  Pallas kernels  13 us (45%)
  starting transfers between devices  9.06 us (32%)
  waiting for transfers between devices  5.74 us (20%)
  other arithmetic  0.65 us (2%)
    ppermute x5, starting transfers between devices, swap(): return lax.ppermute(block, axis, pairs)  9.06 us
    ppermute x5, waiting for transfers between devices, swap(): return lax.ppermute(block, axis, pairs)  5.74 us
    pallas_call x2, Pallas kernels, serve(): call(serve_kernel, shape((rows, heads * width + LANES), bf16), [vmem()] *...  4.82 us
    pallas_call x1, Pallas kernels, shards(): call(own_scores_kernel, (shape((slots, page // 4, 2 * LANES), bf16), shap...  3.62 us
    pallas_call x1, Pallas kernels, shards(): call(own_values_kernel, shape((rows, heads * width), f32), [vmem()] * 5,...  2.2 us
    pallas_call x1, Pallas kernels, shards(): call(pack_kernel, (shape((rows, heads * nope + narrow + LANES), bf16), sh...  1.38 us
    pallas_call x1, Pallas kernels, shards(): call(join_kernel, (shape((rows, cols), bf16), shape((rows, cols), f32)),...  0.99 us
    convert_element_type x1, other arithmetic, shards(): return (kept + swap(sent, 'tp', False).astype(f32)).astype(bf16)  0.65 us
  transfers between devices with their start and end apart: 5, of which 2 were waited for; matrix products, arithmetic and copies ran while one was open for 0% of the time, Pallas kernels for 37%

profile of v1, /device:TPU:0, one launch (start us, length us, event | category | flops | bytes accessed | tf_op | source)
XLA Modules:
  0.0 28.6 jit_solution(6647791108036771062)
XLA Ops:
  0.0 0.0 copy-start
  0.0 0.0 copy-start.2
  0.0 0.0 copy-start.4
  0.0 1.4 %shard_map.100 = (bf16[32,1664]{1,0:T(8,128)(2,1)S(1)}, s32[16,128]{1,0:T(8,128)S(1)}) custom-call(s32[1,32]{1,0:T(1,128)} %bitcast.5, s32[8,32]{1,0:T(8,128)} %bitcast.3, s32[2,32]{1,0:T(2,128)} %bitcast.4, bf16[32,1024]{1,0:T(8,128)(2,1)} %q_nope.1, bf16[32,512]{1,0:T(8,128)(2,1)} %q_rope.1), custom_call_target="tpu_custom_call" | custom-call | flops 20000000000 | bytes 67108864 | tf_op jit(solution)/shard_map/pallas_call | solution.py:470
  1.4 0.0 copy-start.1
  1.4 0.5 %collective-permute-start = (bf16[32,1664]{1,0:T(8,128)(2,1)S(1)}, bf16[32,1664]{1,0:T(8,128)(2,1)S(1)}, u32[]{:S(2)}, u32[]{:S(2)}) collective-permute-start(bf16[32,1664]{1,0:T(8,128)(2,1)S(1)} %get-tuple-element.15.message), channel_id=1, source_target_pairs={{0,2},{2,0},{4,6},{6,4},{8,10},{10,8},{12,14},{14,12},{16,18},{18,... | collective-permute-start | bytes 319496 | tf_op jit(solution)/shard_map/ppermute | solution.py:30
  1.9 5.6 %collective-permute-start.2 = (bf16[32,1664]{1,0:T(8,128)(2,1)S(1)}, bf16[32,1664]{1,0:T(8,128)(2,1)S(1)}, u32[]{:S(2)}, u32[]{:S(2)}) collective-permute-start(bf16[32,1664]{1,0:T(8,128)(2,1)S(1)} %get-tuple-element.15.message), channel_id=1, source_target_pairs={{2,4},{4,2},{6,8},{8,6},{10,12},{12,10},{14,16},{16,14},{18,20},{2... | collective-permute-start | bytes 319496 | tf_op jit(solution)/shard_map/ppermute | solution.py:30
  7.5 0.0 copy-done
  7.5 0.0 copy-done.2
  7.5 0.0 copy-done.4
  7.5 3.6 %shard_map.101 = (bf16[96,16,256]{2,1,0:T(8,128)(2,1)S(1)}, f32[1056,128]{1,0:T(8,128)S(1)}, f32[256,128]{1,0:T(8,128)S(1)}, f32[256,128]{1,0:T(8,128)S(1)}, s32[16,128]{1,0:T(8,128)S(1)}) custom-call(s32[16,128]{1,0:T(8,128)S(1)} %get-tuple-element.14.own, bf16[32,1664]{1,0:T(8,128)(2,1)S(1)} %get-tuple-element.15.message, bf16[96,4096]{1,0:T(8,128)(2,1)S(1)} %copy-done.4, ...), custom_call_target="tpu_custom_call" | custom-call | flops 167772160 | bytes 7864320 | tf_op jit(solution)/shard_map/pallas_call | solution.py:482
  11.2 0.0 collective-permute-done.message
  11.2 0.0 copy-done.1
  11.2 2.1 %shard_map.103 = bf16[32,1152]{1,0:T(8,128)(2,1)S(1)} custom-call(bf16[32,1664]{1,0:T(8,128)(2,1)S(1)} %collective-permute-done.message, bf16[96,64,512]{2,1,0:T(8,128)(2,1)S(1)} %copy-done, bf16[96,16,256]{2,1,0:T(8,128)(2,1)S(1)} %get-tuple-element.20.rope_keys, bf16[8,128,512]{2,1,0:T(8,128)(2,1)S(1)} %copy-done.2, bf16[8,512,128]{2,1,0:T(8,128)(2,1)S(1)} %copy-done.1), custom_call_target="tpu_custom_call" | custom-call | tf_op jit(solution)/shard_map/pallas_call | solution.py:524
  13.2 0.1 collective-permute-start.1
  13.3 0.0 collective-permute-done.2.message
  13.3 2.8 %shard_map.104 = bf16[32,1152]{1,0:T(8,128)(2,1)S(1)} custom-call(bf16[32,1664]{1,0:T(8,128)(2,1)S(1)} %collective-permute-done.2.message, bf16[96,64,512]{2,1,0:T(8,128)(2,1)S(1)} %copy-done, bf16[96,16,256]{2,1,0:T(8,128)(2,1)S(1)} %get-tuple-element.20.rope_keys, bf16[8,128,512]{2,1,0:T(8,128)(2,1)S(1)} %copy-done.2, bf16[8,512,128]{2,1,0:T(8,128)(2,1)S(1)} %copy-done.1), custom_call_target="tpu_custom_call" | custom-call | tf_op jit(solution)/shard_map/pallas_call | solution.py:524
  16.1 0.0 copy-start.3
  16.1 1.3 %collective-permute-start.3 = (bf16[32,1152]{1,0:T(8,128)(2,1)S(1)}, bf16[32,1152]{1,0:T(8,128)(2,1)S(1)}, u32[]{:S(2)}, u32[]{:S(2)}) collective-permute-start(bf16[32,1152]{1,0:T(8,128)(2,1)S(1)} %shard_map.104), channel_id=1, source_target_pairs={{2,4},{4,2},{6,8},{8,6},{10,12},{12,10},{14,16},{16,14},{18,20},{2... | collective-permute-start | bytes 221192 | tf_op jit(solution)/shard_map/ppermute | solution.py:30
  17.4 2.2 %shard_map.102.outs = f32[32,1024]{1,0:T(8,128)S(1)} custom-call(s32[16,128]{1,0:T(8,128)S(1)} %get-tuple-element.16.items, bf16[96,64,512]{2,1,0:T(8,128)(2,1)S(1)} %copy-done, f32[1056,128]{1,0:T(8,128)S(1)} %get-tuple-element.17.weights, f32[256,128]{1,0:T(8,128)S(1)} %get-tuple-element.18.norm, bf16[8,512,128]{2,1,0:T(8,128)(2,1)S(1)} %copy-done.1), custom_call_target="tpu_custom_call" | custom-call | tf_op jit(solution)/shard_map/pallas_call | solution.py:538
  19.6 0.0 collective-permute-done.1.from_a
  19.7 3.0 %collective-permute-done.3.from_b = bf16[32,1152]{1,0:T(8,128)(2,1)S(1)} collective-permute-done((bf16[32,1152]{1,0:T(8,128)(2,1)S(1)}, bf16[32,1152]{1,0:T(8,128)(2,1)S(1)}, u32[]{:S(2)}, u32[]{:S(2)}) %collective-permute-start.3) | collective-permute-done | bytes 73760 | tf_op jit(solution)/shard_map/ppermute | solution.py:30
  22.7 0.0 copy-done.3
  22.7 1.0 %shard_map.105 = (bf16[32,1024]{1,0:T(8,128)(2,1)S(1)}, f32[32,1024]{1,0:T(8,128)S(1)}) custom-call(f32[32,1024]{1,0:T(8,128)S(1)} %shard_map.102.outs, f32[256,128]{1,0:T(8,128)S(1)} %get-tuple-element.19.lse, bf16[32,1152]{1,0:T(8,128)(2,1)S(1)} %collective-permute-done.1.from_a, bf16[32,1152]{1,0:T(8,128)(2,1)S(1)} %collective-permute-done.3.from_b, ...), custom_call_target="tpu_custom_call" | custom-call | tf_op jit(solution)/shard_map/pallas_call | solution.py:547
  23.6 1.5 %collective-permute-start.4 = (bf16[32,1024]{1,0:T(8,128)(2,1)S(1)}, bf16[32,1024]{1,0:T(8,128)(2,1)S(1)}, u32[]{:S(2)}, u32[]{:S(2)}) collective-permute-start(bf16[32,1024]{1,0:T(8,128)(2,1)S(1)} %get-tuple-element.22), channel_id=1, source_target_pairs={{0,1},{1,0},{2,3},{3,2},{4,5},{5,4},{6,7},{7,6},{8,9},{9,8},{10,11... | collective-permute-start | bytes 196616 | tf_op jit(solution)/shard_map/ppermute | solution.py:30
  25.2 2.7 %collective-permute-done.4 = bf16[32,1024]{1,0:T(8,128)(2,1)S(1)} collective-permute-done((bf16[32,1024]{1,0:T(8,128)(2,1)S(1)}, bf16[32,1024]{1,0:T(8,128)(2,1)S(1)}, u32[]{:S(2)}, u32[]{:S(2)}) %collective-permute-start.4) | collective-permute-done | bytes 65568 | tf_op jit(solution)/shard_map/ppermute | solution.py:30
  27.9 0.6 %add_convert_fusion = bf16[32,1024]{1,0:T(8,128)(2,1)} fusion(f32[32,1024]{1,0:T(8,128)S(1)} %get-tuple-element.21, bf16[32,1024]{1,0:T(8,128)(2,1)S(1)} %collective-permute-done.4), kind=kLoop, calls=%fused_computation | loop fusion | flops 98304 | bytes 262144 | tf_op jit(solution)/shard_map/convert_element_type | solution.py:555
Async XLA Ops:
  0.0 7.5 %copy-start = (bf16[96,64,512]{2,1,0:T(8,128)(2,1)S(1)}, bf16[96,64,512]{2,1,0:T(8,128)(2,1)}, u32[]{:S(2)}) copy-start(bf16[96,64,512]{2,1,0:T(8,128)(2,1)} %pool.7) | copy-start | bytes 18874372
  0.0 7.5 %copy-start.2 = (bf16[8,128,512]{2,1,0:T(8,128)(2,1)S(1)}, bf16[8,128,512]{2,1,0:T(8,128)(2,1)}, u32[]{:S(2)}) copy-start(bf16[8,128,512]{2,1,0:T(8,128)(2,1)} %w_uk.5) | copy-start | bytes 3145732
  0.0 7.5 %copy-start.4 = (bf16[96,4096]{1,0:T(8,128)(2,1)S(1)}, bf16[96,4096]{1,0:T(8,128)(2,1)}, u32[]{:S(2)}) copy-start(bf16[96,4096]{1,0:T(8,128)(2,1)} %rope_pages.1) | copy-start | bytes 2359300
  1.4 9.8 %copy-start.1 = (bf16[8,512,128]{2,1,0:T(8,128)(2,1)S(1)}, bf16[8,512,128]{2,1,0:T(8,128)(2,1)}, u32[]{:S(2)}) copy-start(bf16[8,512,128]{2,1,0:T(8,128)(2,1)} %w_uv.5) | copy-start | bytes 3145732
  1.4 9.8 %collective-permute-start = (bf16[32,1664]{1,0:T(8,128)(2,1)S(1)}, bf16[32,1664]{1,0:T(8,128)(2,1)S(1)}, u32[]{:S(2)}, u32[]{:S(2)}) collective-permute-start(bf16[32,1664]{1,0:T(8,128)(2,1)S(1)} %get-tuple-element.15.message), channel_id=1, source_target_pairs={{0,2},{2,0},{4,6},{6,4},{8,10},{10,8},{12,14},{14,12},{16,18},{18,... | collective-permute-start | bytes 319496 | tf_op jit(solution)/shard_map/ppermute | solution.py:30
  1.9 11.4 %collective-permute-start.2 = (bf16[32,1664]{1,0:T(8,128)(2,1)S(1)}, bf16[32,1664]{1,0:T(8,128)(2,1)S(1)}, u32[]{:S(2)}, u32[]{:S(2)}) collective-permute-start(bf16[32,1664]{1,0:T(8,128)(2,1)S(1)} %get-tuple-element.15.message), channel_id=1, source_target_pairs={{2,4},{4,2},{6,8},{8,6},{10,12},{12,10},{14,16},{16,14},{18,20},{2... | collective-permute-start | bytes 319496 | tf_op jit(solution)/shard_map/ppermute | solution.py:30
  13.2 6.4 %collective-permute-start.1 = (bf16[32,1152]{1,0:T(8,128)(2,1)S(1)}, bf16[32,1152]{1,0:T(8,128)(2,1)S(1)}, u32[]{:S(2)}, u32[]{:S(2)}) collective-permute-start(bf16[32,1152]{1,0:T(8,128)(2,1)S(1)} %shard_map.103), channel_id=1, source_target_pairs={{0,2},{2,0},{4,6},{6,4},{8,10},{10,8},{12,14},{14,12},{16,18},{18,... | collective-permute-start | bytes 221192 | tf_op jit(solution)/shard_map/ppermute | solution.py:30
  16.1 6.6 %copy-start.3 = (bf16[1024,2048]{1,0:T(8,128)(2,1)S(1)}, bf16[1024,2048]{1,0:T(8,128)(2,1)}, u32[]{:S(2)}) copy-start(bf16[1024,2048]{1,0:T(8,128)(2,1)} %w_o.1) | copy-start | bytes 12582916
  16.1 6.5 %collective-permute-start.3 = (bf16[32,1152]{1,0:T(8,128)(2,1)S(1)}, bf16[32,1152]{1,0:T(8,128)(2,1)S(1)}, u32[]{:S(2)}, u32[]{:S(2)}) collective-permute-start(bf16[32,1152]{1,0:T(8,128)(2,1)S(1)} %shard_map.104), channel_id=1, source_target_pairs={{2,4},{4,2},{6,8},{8,6},{10,12},{12,10},{14,16},{16,14},{18,20},{2... | collective-permute-start | bytes 221192 | tf_op jit(solution)/shard_map/ppermute | solution.py:30
  23.6 4.3 %collective-permute-start.4 = (bf16[32,1024]{1,0:T(8,128)(2,1)S(1)}, bf16[32,1024]{1,0:T(8,128)(2,1)S(1)}, u32[]{:S(2)}, u32[]{:S(2)}) collective-permute-start(bf16[32,1024]{1,0:T(8,128)(2,1)S(1)} %get-tuple-element.22), channel_id=1, source_target_pairs={{0,1},{1,0},{2,3},{3,2},{4,5},{5,4},{6,7},{7,6},{8,9},{9,8},{10,11... | collective-permute-start | bytes 196616 | tf_op jit(solution)/shard_map/ppermute | solution.py:30

commit v2 on v1

--- a/solution.py
+++ b/solution.py
@@ -118,12 +118,26 @@
     nope = w_uk.shape[1]
     tiles = latent // LANES
     low = lax.broadcasted_iota(jnp.int32, (rows, LANES), 1) < LANES // 2
-    for h in range(heads):
-        lat = jnp.dot(
-            message[:, h * nope : (h + 1) * nope], w_uk[h], preferred_element_type=jnp.float32
+    for h in range(0, heads, 2):
+        first = message[:, h * nope : (h + 1) * nope]
+        second = message[:, (h + 1) * nope : (h + 2) * nope]
+        none = jnp.zeros_like(first)
+        both = jnp.dot(
+            jnp.concatenate(
+                [
+                    jnp.concatenate([first, none], axis=1),
+                    jnp.concatenate([none, second], axis=1),
+                ],
+                axis=0,
+            ),
+            jnp.concatenate([w_uk[h], w_uk[h + 1]], axis=0),
+            preferred_element_type=jnp.float32,
         )
-        for c in range(tiles):
-            queries[c, pl.ds(h, rows, stride=heads), :] = lat[:, c * LANES : (c + 1) * LANES]
+        for k in range(2):
+            for c in range(tiles):
+                queries[c, pl.ds(h + k, rows, stride=heads), :] = both[
+                    k * rows : (k + 1) * rows, c * LANES : (c + 1) * LANES
+                ]
     for c in range(narrow // LANES):
         pair = lane_tile(message, heads * nope // LANES + c).astype(jnp.float32)
         swapped = pltpu.roll(pair, LANES // 2, 1)
@@ -310,6 +324,14 @@
         )
         yield h, both[:rows, :width]
         yield h + 1, both[rows:, width:]
+
+
+def heads_in_lanes(lse, rows, heads):
+    lane = lax.rem(lax.broadcasted_iota(jnp.int32, (rows, LANES), 1), heads)
+    logs = jnp.zeros((rows, LANES), jnp.float32)
+    for h in range(heads):
+        logs = jnp.where(lane == h, lse[pl.ds(h, rows, stride=heads), :], logs)
+    return logs
 
 
 def own_scores_kernel(
@@ -350,10 +372,13 @@
     soften(scores, weights, norm, lse, rows * heads)
 
 
-def own_values_kernel(items, pool, weights, norm, w_uv, outs, context, plan, plan_sem, *, heads):
+def own_values_kernel(
+    items, pool, weights, norm, lse, w_uv, outs, logs, context, plan, plan_sem, *, heads
+):
     rows = outs.shape[0]
     table = fetch_rows(items, plan, plan_sem)
     context[...] = jnp.zeros_like(context)
+    logs[...] = heads_in_lanes(lse, rows, heads)
     for copy in table:
         copy.wait()
     value_work(pool, weights, context, plan, 0, heads, True)
@@ -383,10 +408,9 @@
     value_work(pool, weights, context, plan, base, heads, False)
     width = w_uv.shape[2]
     lane = lax.broadcasted_iota(jnp.int32, (rows, LANES), 1)
-    logs = jnp.zeros((rows, LANES), jnp.float32)
     for h, out in head_outs(context, norm, w_uv, rows, heads):
         back[:, h * width : (h + 1) * width] = out.astype(jnp.bfloat16)
-        logs = jnp.where(lax.rem(lane, heads) == h, lse[pl.ds(h, rows, stride=heads), :], logs)
+    logs = heads_in_lanes(lse, rows, heads)
     packed = jnp.zeros((rows, LANES), jnp.float32)
     for part in range(3):
         piece = logs.astype(jnp.bfloat16).astype(jnp.float32)
@@ -395,35 +419,38 @@
     back[:, heads * width :] = packed.astype(jnp.bfloat16)
 
 
-def join_kernel(outs, lse, from_a, from_b, w_o, sent, kept, joined, *, heads):
+def join_kernel(outs, logs, from_a, from_b, w_o, sent, joined, *, heads):
     rows = outs.shape[0]
     width = outs.shape[1] // heads
-    totals = []
+    logs = [logs[...]]
     for arrived in (from_a, from_b):
         tile = arrived[:, heads * width :].astype(jnp.float32)
-        total = tile + pltpu.roll(tile, LANES - heads, 1) + pltpu.roll(tile, LANES - 2 * heads, 1)
-        totals.append(total)
+        logs.append(
+            tile + pltpu.roll(tile, LANES - heads, 1) + pltpu.roll(tile, LANES - 2 * heads, 1)
+        )
+    peak = jnp.maximum(jnp.maximum(logs[0], logs[1]), logs[2])
+    shares = [jnp.exp(one - peak) for one in logs]
+    whole = 1.0 / (shares[0] + shares[1] + shares[2])
+    shares = [share * whole for share in shares]
     for h in range(heads):
         at = slice(h * width, (h + 1) * width)
-        logs = [lse[pl.ds(h, rows, stride=heads), :]]
-        values = [outs[:, at]]
-        for arrived, total in zip((from_a, from_b), totals):
-            logs.append(jnp.broadcast_to(total[:, h : h + 1], (rows, LANES)))
-            values.append(arrived[:, at].astype(jnp.float32))
-        peak = jnp.maximum(jnp.maximum(logs[0], logs[1]), logs[2])
-        shares = [jnp.exp(one - peak) for one in logs]
-        top = shares[0] * values[0] + shares[1] * values[1] + shares[2] * values[2]
-        joined[:, at] = (top / (shares[0] + shares[1] + shares[2])).astype(jnp.bfloat16)
-    mine = lax.axis_index("tp")
-    other = lax.rem(mine + 1, lax.axis_size("tp"))
-    cols = sent.shape[1]
-    heads_joined = joined[...]
-    away = pl.ds(pl.multiple_of(other * cols, cols), cols)
-    here = pl.ds(pl.multiple_of(mine * cols, cols), cols)
-    sent[...] = jnp.dot(
-        heads_joined, w_o[:, away], preferred_element_type=jnp.float32
-    ).astype(jnp.bfloat16)
-    kept[...] = jnp.dot(heads_joined, w_o[:, here], preferred_element_type=jnp.float32)
+        top = 0.0
+        for values, share in zip((outs, from_a, from_b), shares):
+            mine = jnp.broadcast_to(share[:, h : h + 1], (rows, width))
+            top = top + mine * values[:, at].astype(jnp.float32)
+        joined[:, at] = top.astype(jnp.bfloat16)
+    other = lax.rem(lax.axis_index("tp") + 1, lax.axis_size("tp"))
+    project_out(joined, w_o, other, sent)
+
+
+def project_out(joined, w_o, part, out):
+    cols = out.shape[1]
+    at = pl.ds(pl.multiple_of(part * cols, cols), cols)
+    out[...] = jnp.dot(joined[...], w_o[:, at], preferred_element_type=jnp.float32).astype(out.dtype)
+
+
+def keep_kernel(joined, w_o, kept):
+    project_out(joined, w_o, lax.axis_index("tp"), kept)
 
 
 def vmem():
@@ -535,24 +562,26 @@
     from_b = swap(back_b, "dp", True)
     back_a = serve(asked_a, 0)
     from_a = swap(back_a, "dp", False)
-    outs = call(
+    outs, logs = call(
         own_values_kernel,
-        shape((rows, heads * width), f32),
-        [vmem()] * 5,
+        (shape((rows, heads * width), f32), shape((rows, LANES), f32)),
+        [vmem()] * 6,
         [contexts, plan, sem((TABLE_ROWS,))],
         8,
         heads=heads,
-    )(items, latent_pages, weights, norm, w_uv)
+    )(items, latent_pages, weights, norm, lse, w_uv)
     cols = w_o.shape[1] // lax.axis_size("tp")
-    sent, kept = call(
+    sent, joined = call(
         join_kernel,
-        (shape((rows, cols), bf16), shape((rows, cols), f32)),
+        (shape((rows, cols), bf16), shape((rows, heads * width), bf16)),
         [vmem()] * 5,
-        [pltpu.VMEM((rows, heads * width), bf16)],
+        [],
         8,
         heads=heads,
-    )(outs, lse, from_a, from_b, w_o)
-    return (kept + swap(sent, "tp", False).astype(f32)).astype(bf16)
+    )(outs, logs, from_a, from_b, w_o)
+    arrived = swap(sent, "tp", False)
+    kept = call(keep_kernel, shape((rows, cols), f32), [vmem()] * 2, [], 8)(joined, w_o)
+    return (kept + arrived.astype(f32)).astype(bf16)
 
 
 def solution(mesh):

time: 28.7 us -> 28.4 us (0.990)
  waiting for transfers between devices: 5.74 us -> 5.29 us
    ppermute x5, waiting for transfers between devices: 5.74 us -> 5.29 us  [swap(): return lax.ppermute(block, axis, pairs)]
    pallas_call x2 -> x3, Pallas kernels: 3.19 us -> 3.25 us  [the longest x1 2.2 us: shards(): call(own_values_kernel, (shape((rows, heads * width), f32), shape((rows,...]
  transfers between devices with their start and end apart: 5 -> 5, of which waited for: 2 -> 2; matrix products, arithmetic and copies ran while one was open for 0% -> 0% of each run, Pallas kernels for 37% -> 40%
where the time goes in v2:
time: 28.4 us; the launch traced here: 28.2 us
  Pallas kernels  13.1 us (46%)
  starting transfers between devices  9.06 us (32%)
  waiting for transfers between devices  5.29 us (19%)
  other arithmetic  0.64 us (2%)
    ppermute x5, starting transfers between devices, swap(): return lax.ppermute(block, axis, pairs)  9.06 us
    ppermute x5, waiting for transfers between devices, swap(): return lax.ppermute(block, axis, pairs)  5.29 us
    pallas_call x2, Pallas kernels, serve(): call(serve_kernel, shape((rows, heads * width + LANES), bf16), [vmem()] *...  4.84 us
    pallas_call x1, Pallas kernels, shards(): call(own_scores_kernel, (shape((slots, page // 4, 2 * LANES), bf16), shap...  3.65 us
    pallas_call x1, Pallas kernels, shards(): call(own_values_kernel, (shape((rows, heads * width), f32), shape((rows,...  2.2 us
    pallas_call x1, Pallas kernels, shards(): call(pack_kernel, (shape((rows, heads * nope + narrow + LANES), bf16), sh...  1.38 us
    convert_element_type x1, other arithmetic, shards(): return (kept + arrived.astype(f32)).astype(bf16)  0.64 us
    pallas_call x1, Pallas kernels, shards(): call(join_kernel, (shape((rows, cols), bf16), shape((rows, heads * width)...  0.6 us
  transfers between devices with their start and end apart: 5, of which 2 were waited for; matrix products, arithmetic and copies ran while one was open for 0% of the time, Pallas kernels for 40%

profile of v2, /device:TPU:0, one launch (start us, length us, event | category | flops | bytes accessed | tf_op | source)
XLA Modules:
  0.0 28.2 jit_solution(6311487466193546522)
XLA Ops:
  0.0 0.0 copy-start
  0.0 0.0 copy-start.3
  0.0 0.0 copy-start.4
  0.0 1.4 %shard_map.100 = (bf16[32,1664]{1,0:T(8,128)(2,1)S(1)}, s32[16,128]{1,0:T(8,128)S(1)}) custom-call(s32[1,32]{1,0:T(1,128)} %bitcast.5, s32[8,32]{1,0:T(8,128)} %bitcast.3, s32[2,32]{1,0:T(2,128)} %bitcast.4, bf16[32,1024]{1,0:T(8,128)(2,1)} %q_nope.1, bf16[32,512]{1,0:T(8,128)(2,1)} %q_rope.1), custom_call_target="tpu_custom_call" | custom-call | flops 20000000000 | bytes 67108864 | tf_op jit(solution)/shard_map/pallas_call | solution.py:497
  1.4 0.0 copy-start.2
  1.4 0.5 %collective-permute-start = (bf16[32,1664]{1,0:T(8,128)(2,1)S(1)}, bf16[32,1664]{1,0:T(8,128)(2,1)S(1)}, u32[]{:S(2)}, u32[]{:S(2)}) collective-permute-start(bf16[32,1664]{1,0:T(8,128)(2,1)S(1)} %get-tuple-element.17.message), channel_id=1, source_target_pairs={{0,2},{2,0},{4,6},{6,4},{8,10},{10,8},{12,14},{14,12},{16,18},{18,... | collective-permute-start | bytes 319496 | tf_op jit(solution)/shard_map/ppermute | solution.py:30
  1.9 5.6 %collective-permute-start.2 = (bf16[32,1664]{1,0:T(8,128)(2,1)S(1)}, bf16[32,1664]{1,0:T(8,128)(2,1)S(1)}, u32[]{:S(2)}, u32[]{:S(2)}) collective-permute-start(bf16[32,1664]{1,0:T(8,128)(2,1)S(1)} %get-tuple-element.17.message), channel_id=1, source_target_pairs={{2,4},{4,2},{6,8},{8,6},{10,12},{12,10},{14,16},{16,14},{18,20},{2... | collective-permute-start | bytes 319496 | tf_op jit(solution)/shard_map/ppermute | solution.py:30
  7.5 0.0 copy-done
  7.5 0.0 copy-done.3
  7.5 0.0 copy-done.4
  7.5 3.6 %shard_map.101 = (bf16[96,16,256]{2,1,0:T(8,128)(2,1)S(1)}, f32[1056,128]{1,0:T(8,128)S(1)}, f32[256,128]{1,0:T(8,128)S(1)}, f32[256,128]{1,0:T(8,128)S(1)}, s32[16,128]{1,0:T(8,128)S(1)}) custom-call(s32[16,128]{1,0:T(8,128)S(1)} %get-tuple-element.16.own, bf16[32,1664]{1,0:T(8,128)(2,1)S(1)} %get-tuple-element.17.message, bf16[96,4096]{1,0:T(8,128)(2,1)S(1)} %copy-done.4, ...), custom_call_target="tpu_custom_call" | custom-call | flops 167772160 | bytes 7864320 | tf_op jit(solution)/shard_map/pallas_call | solution.py:509
  11.2 0.0 collective-permute-done.message
  11.2 0.0 copy-done.2
  11.2 2.1 %shard_map.103 = bf16[32,1152]{1,0:T(8,128)(2,1)S(1)} custom-call(bf16[32,1664]{1,0:T(8,128)(2,1)S(1)} %collective-permute-done.message, bf16[96,64,512]{2,1,0:T(8,128)(2,1)S(1)} %copy-done, bf16[96,16,256]{2,1,0:T(8,128)(2,1)S(1)} %get-tuple-element.24.rope_keys, bf16[8,128,512]{2,1,0:T(8,128)(2,1)S(1)} %copy-done.3, bf16[8,512,128]{2,1,0:T(8,128)(2,1)S(1)} %copy-done.2), custom_call_target="tpu_custom_call" | custom-call | tf_op jit(solution)/shard_map/pallas_call | solution.py:551
  13.3 0.1 collective-permute-start.1
  13.4 0.0 collective-permute-done.2.message
  13.4 2.8 %shard_map.104 = bf16[32,1152]{1,0:T(8,128)(2,1)S(1)} custom-call(bf16[32,1664]{1,0:T(8,128)(2,1)S(1)} %collective-permute-done.2.message, bf16[96,64,512]{2,1,0:T(8,128)(2,1)S(1)} %copy-done, bf16[96,16,256]{2,1,0:T(8,128)(2,1)S(1)} %get-tuple-element.24.rope_keys, bf16[8,128,512]{2,1,0:T(8,128)(2,1)S(1)} %copy-done.3, bf16[8,512,128]{2,1,0:T(8,128)(2,1)S(1)} %copy-done.2), custom_call_target="tpu_custom_call" | custom-call | tf_op jit(solution)/shard_map/pallas_call | solution.py:551
  16.1 0.0 copy-start.1
  16.2 1.3 %collective-permute-start.3 = (bf16[32,1152]{1,0:T(8,128)(2,1)S(1)}, bf16[32,1152]{1,0:T(8,128)(2,1)S(1)}, u32[]{:S(2)}, u32[]{:S(2)}) collective-permute-start(bf16[32,1152]{1,0:T(8,128)(2,1)S(1)} %shard_map.104), channel_id=1, source_target_pairs={{2,4},{4,2},{6,8},{8,6},{10,12},{12,10},{14,16},{16,14},{18,20},{2... | collective-permute-start | bytes 221192 | tf_op jit(solution)/shard_map/ppermute | solution.py:30
  17.5 2.2 %shard_map.102 = (f32[32,1024]{1,0:T(8,128)S(1)}, f32[32,128]{1,0:T(8,128)S(1)}) custom-call(s32[16,128]{1,0:T(8,128)S(1)} %get-tuple-element.18.items, bf16[96,64,512]{2,1,0:T(8,128)(2,1)S(1)} %copy-done, f32[1056,128]{1,0:T(8,128)S(1)} %get-tuple-element.19.weights, f32[256,128]{1,0:T(8,128)S(1)} %get-tuple-element.20.norm, ...), custom_call_target="tpu_custom_call" | custom-call | tf_op jit(solution)/shard_map/pallas_call | solution.py:565
  19.7 0.0 collective-permute-done.1.from_a
  19.7 3.0 %collective-permute-done.3.from_b = bf16[32,1152]{1,0:T(8,128)(2,1)S(1)} collective-permute-done((bf16[32,1152]{1,0:T(8,128)(2,1)S(1)}, bf16[32,1152]{1,0:T(8,128)(2,1)S(1)}, u32[]{:S(2)}, u32[]{:S(2)}) %collective-permute-start.3) | collective-permute-done | bytes 73760 | tf_op jit(solution)/shard_map/ppermute | solution.py:30
  22.7 0.0 copy-done.1
  22.7 0.6 %shard_map.105 = (bf16[32,1024]{1,0:T(8,128)(2,1)S(1)}, bf16[32,1024]{1,0:T(8,128)(2,1)S(1)}) custom-call(f32[32,1024]{1,0:T(8,128)S(1)} %get-tuple-element.22.outs, f32[32,128]{1,0:T(8,128)S(1)} %get-tuple-element.23.logs, bf16[32,1152]{1,0:T(8,128)(2,1)S(1)} %collective-permute-done.1.from_a, bf16[32,1152]{1,0:T(8,128)(2,1)S(1)} %collective-permute-done.3.from_b, ...), custom_call_target="tpu_custom_call" | custom-call | tf_op jit(solution)/shard_map/pallas_call | solution.py:574
  23.3 1.5 %collective-permute-start.4 = (bf16[32,1024]{1,0:T(8,128)(2,1)S(1)}, bf16[32,1024]{1,0:T(8,128)(2,1)S(1)}, u32[]{:S(2)}, u32[]{:S(2)}) collective-permute-start(bf16[32,1024]{1,0:T(8,128)(2,1)S(1)} %get-tuple-element.26), channel_id=1, source_target_pairs={{0,1},{1,0},{2,3},{3,2},{4,5},{5,4},{6,7},{7,6},{8,9},{9,8},{10,11... | collective-permute-start | bytes 196616 | tf_op jit(solution)/shard_map/ppermute | solution.py:30
  24.8 0.5 %shard_map.106 = f32[32,1024]{1,0:T(8,128)S(1)} custom-call(bf16[32,1024]{1,0:T(8,128)(2,1)S(1)} %get-tuple-element.25.joined, bf16[1024,2048]{1,0:T(8,128)(2,1)S(1)} %copy-done.1), custom_call_target="tpu_custom_call" | custom-call | tf_op jit(solution)/shard_map/pallas_call | solution.py:583
  25.3 2.3 %collective-permute-done.4 = bf16[32,1024]{1,0:T(8,128)(2,1)S(1)} collective-permute-done((bf16[32,1024]{1,0:T(8,128)(2,1)S(1)}, bf16[32,1024]{1,0:T(8,128)(2,1)S(1)}, u32[]{:S(2)}, u32[]{:S(2)}) %collective-permute-start.4) | collective-permute-done | bytes 65568 | tf_op jit(solution)/shard_map/ppermute | solution.py:30
  27.6 0.6 %add_convert_fusion = bf16[32,1024]{1,0:T(8,128)(2,1)} fusion(f32[32,1024]{1,0:T(8,128)S(1)} %shard_map.106, bf16[32,1024]{1,0:T(8,128)(2,1)S(1)} %collective-permute-done.4), kind=kLoop, calls=%fused_computation | loop fusion | flops 98304 | bytes 262144 | tf_op jit(solution)/shard_map/convert_element_type | solution.py:584
Async XLA Ops:
  0.0 7.5 %copy-start = (bf16[96,64,512]{2,1,0:T(8,128)(2,1)S(1)}, bf16[96,64,512]{2,1,0:T(8,128)(2,1)}, u32[]{:S(2)}) copy-start(bf16[96,64,512]{2,1,0:T(8,128)(2,1)} %pool.7) | copy-start | bytes 18874372
  0.0 7.5 %copy-start.3 = (bf16[8,128,512]{2,1,0:T(8,128)(2,1)S(1)}, bf16[8,128,512]{2,1,0:T(8,128)(2,1)}, u32[]{:S(2)}) copy-start(bf16[8,128,512]{2,1,0:T(8,128)(2,1)} %w_uk.5) | copy-start | bytes 3145732
  0.0 7.5 %copy-start.4 = (bf16[96,4096]{1,0:T(8,128)(2,1)S(1)}, bf16[96,4096]{1,0:T(8,128)(2,1)}, u32[]{:S(2)}) copy-start(bf16[96,4096]{1,0:T(8,128)(2,1)} %rope_pages.1) | copy-start | bytes 2359300
  1.4 9.8 %copy-start.2 = (bf16[8,512,128]{2,1,0:T(8,128)(2,1)S(1)}, bf16[8,512,128]{2,1,0:T(8,128)(2,1)}, u32[]{:S(2)}) copy-start(bf16[8,512,128]{2,1,0:T(8,128)(2,1)} %w_uv.5) | copy-start | bytes 3145732
  1.4 9.8 %collective-permute-start = (bf16[32,1664]{1,0:T(8,128)(2,1)S(1)}, bf16[32,1664]{1,0:T(8,128)(2,1)S(1)}, u32[]{:S(2)}, u32[]{:S(2)}) collective-permute-start(bf16[32,1664]{1,0:T(8,128)(2,1)S(1)} %get-tuple-element.17.message), channel_id=1, source_target_pairs={{0,2},{2,0},{4,6},{6,4},{8,10},{10,8},{12,14},{14,12},{16,18},{18,... | collective-permute-start | bytes 319496 | tf_op jit(solution)/shard_map/ppermute | solution.py:30
  1.9 11.5 %collective-permute-start.2 = (bf16[32,1664]{1,0:T(8,128)(2,1)S(1)}, bf16[32,1664]{1,0:T(8,128)(2,1)S(1)}, u32[]{:S(2)}, u32[]{:S(2)}) collective-permute-start(bf16[32,1664]{1,0:T(8,128)(2,1)S(1)} %get-tuple-element.17.message), channel_id=1, source_target_pairs={{2,4},{4,2},{6,8},{8,6},{10,12},{12,10},{14,16},{16,14},{18,20},{2... | collective-permute-start | bytes 319496 | tf_op jit(solution)/shard_map/ppermute | solution.py:30
  13.3 6.4 %collective-permute-start.1 = (bf16[32,1152]{1,0:T(8,128)(2,1)S(1)}, bf16[32,1152]{1,0:T(8,128)(2,1)S(1)}, u32[]{:S(2)}, u32[]{:S(2)}) collective-permute-start(bf16[32,1152]{1,0:T(8,128)(2,1)S(1)} %shard_map.103), channel_id=1, source_target_pairs={{0,2},{2,0},{4,6},{6,4},{8,10},{10,8},{12,14},{14,12},{16,18},{18,... | collective-permute-start | bytes 221192 | tf_op jit(solution)/shard_map/ppermute | solution.py:30
  16.1 6.6 %copy-start.1 = (bf16[1024,2048]{1,0:T(8,128)(2,1)S(1)}, bf16[1024,2048]{1,0:T(8,128)(2,1)}, u32[]{:S(2)}) copy-start(bf16[1024,2048]{1,0:T(8,128)(2,1)} %w_o.3) | copy-start | bytes 12582916
  16.2 6.5 %collective-permute-start.3 = (bf16[32,1152]{1,0:T(8,128)(2,1)S(1)}, bf16[32,1152]{1,0:T(8,128)(2,1)S(1)}, u32[]{:S(2)}, u32[]{:S(2)}) collective-permute-start(bf16[32,1152]{1,0:T(8,128)(2,1)S(1)} %shard_map.104), channel_id=1, source_target_pairs={{2,4},{4,2},{6,8},{8,6},{10,12},{12,10},{14,16},{16,14},{18,20},{2... | collective-permute-start | bytes 221192 | tf_op jit(solution)/shard_map/ppermute | solution.py:30
  23.3 4.3 %collective-permute-start.4 = (bf16[32,1024]{1,0:T(8,128)(2,1)S(1)}, bf16[32,1024]{1,0:T(8,128)(2,1)S(1)}, u32[]{:S(2)}, u32[]{:S(2)}) collective-permute-start(bf16[32,1024]{1,0:T(8,128)(2,1)S(1)} %get-tuple-element.26), channel_id=1, source_target_pairs={{0,1},{1,0},{2,3},{3,2},{4,5},{5,4},{6,7},{7,6},{8,9},{9,8},{10,11... | collective-permute-start | bytes 196616 | tf_op jit(solution)/shard_map/ppermute | solution.py:30

commit v3 on v2

--- a/solution.py
+++ b/solution.py
@@ -65,11 +65,28 @@
     return moved, count
 
 
-def pack_kernel(lengths, table, lend, q_nope, q_rope, message, own, fields, *, page):
+def pack_kernel(
+    lengths_hbm, table_hbm, lend_hbm, q_nope, q_rope,
+    message, own,
+    lengths, table, lend, fields, sems,
+    *, page,
+):
     rows = q_nope.shape[0]
     most = table.shape[0]
     shift = page.bit_length() - 1
     wide, narrow = q_nope.shape[1], q_rope.shape[1]
+    routes = (
+        (lengths_hbm, lengths),
+        (table_hbm, table),
+        (lend_hbm, lend),
+        (q_nope, message.at[:, pl.ds(0, wide)]),
+        (q_rope, message.at[:, pl.ds(wide, narrow)]),
+    )
+    copies = [pltpu.make_async_copy(*route, sems.at[k]) for k, route in enumerate(routes)]
+    for copy in copies:
+        copy.start()
+    for copy in copies[:3]:
+        copy.wait()
     length = lengths[...]
     count = lax.shift_right_logical(length + (page - 1), shift)
     to_prev, to_next = lend[0:1, :], lend[1:2, :]
@@ -103,14 +120,14 @@
     moved, counts = compact(fields[...], LIVE, rows, LANES // 2)
     row = lax.broadcasted_iota(jnp.int32, (FIELDS, LANES), 0)
     asked = jnp.where(row == COUNT, counts, moved).astype(message.dtype)
-    message[:, :wide] = q_nope[...]
-    message[:, wide : wide + narrow] = q_rope[...]
     message[:, wide + narrow :] = jnp.concatenate(
         [asked, jnp.zeros((rows - FIELDS, LANES), message.dtype)], axis=0
     )
     own[...] = jnp.zeros_like(own)
     mine = [pick(jnp.minimum(k, held - 1)) for k in range(most)]
     own[:, :rows] = stack([*mine, jnp.minimum(length, held * page)], FIELDS)
+    for copy in copies[3:]:
+        copy.wait()
 
 
 def project_queries(message, w_uk, queries, heads, latent, narrow):
@@ -135,14 +152,14 @@
         )
         for k in range(2):
             for c in range(tiles):
-                queries[c, pl.ds(h + k, rows, stride=heads), :] = both[
+                queries[c, pl.ds(h + k, rows, stride=heads + 1), :] = both[
                     k * rows : (k + 1) * rows, c * LANES : (c + 1) * LANES
                 ]
     for c in range(narrow // LANES):
         pair = lane_tile(message, heads * nope // LANES + c).astype(jnp.float32)
         swapped = pltpu.roll(pair, LANES // 2, 1)
         for h, left, right in ((2 * c, pair, swapped), (2 * c + 1, swapped, pair)):
-            at = pl.ds(h, rows, stride=heads)
+            at = pl.ds(h, rows, stride=heads + 1)
             queries[tiles, at, :] = jnp.where(low, left, 0.0)
             queries[tiles + 1, at, :] = jnp.where(low, 0.0, right)
 
@@ -150,14 +167,14 @@
 def to_table(moved, count, rows, heads, score_row=None):
     whole = moved.astype(jnp.int32)
     request = whole[ROW : ROW + 1, :]
-    query_row = jnp.where(request == 0, rows, request - 1) * heads
+    query_row = jnp.where(request == 0, rows, request - 1)
     blocks = lax.shift_right_logical(
         count[0:1, :].astype(jnp.int32) + (UNROLL - 1), UNROLL.bit_length() - 1
     )
     row = lax.broadcasted_iota(jnp.int32, whole.shape, 0)
-    for k, value in ((ROW, query_row), (COUNT, blocks)):
+    for k, value in ((ROW, query_row * (heads + 1)), (COUNT, blocks)):
         whole = jnp.where(row == k, jnp.broadcast_to(value, whole.shape), whole)
-    extra = query_row if score_row is None else query_row + score_row(whole)
+    extra = query_row * heads if score_row is None else query_row * heads + score_row(whole)
     return jnp.where(row == SCORE_ROW, jnp.broadcast_to(extra, whole.shape), whole)
 
 
@@ -225,42 +242,56 @@
     return copies
 
 
-def read(plan, row, at):
-    return plan[row * LANES + at]
-
-
-def item(plan, at, heads):
-    slots = [read(plan, k, at) for k in range(LEND)]
-    return pl.multiple_of(read(plan, ROW, at), heads), slots
-
-
-def score_work(queries, pool, rope_keys, scores, plan, base, heads, scale):
+def from_plan(plan, first):
+    return lambda row, u: plan[row * LANES + first + u]
+
+
+def from_table(items, base):
+    table = items[0:8, :]
+    return lambda row, u: table[row, base + u]
+
+
+def each_block(plan, items, copies, base, work):
+    done = 0
+    if items is not None:
+        work(from_table(items, base))
+        done = 1
+    for copy in copies:
+        copy.wait()
+
+    @pl.loop(done, plan[COUNT * LANES + base])
+    def _(block):
+        work(from_plan(plan, base + block * UNROLL))
+
+
+def score_work(queries, pool, rope_keys, scores, plan, items, copies, base, heads, scale):
     page = pool.shape[1]
     scores[...] = jnp.full_like(scores, FAR)
     position = lax.broadcasted_iota(jnp.int32, (heads, LEND * page), 1)
     lanes = rope_lanes(page, heads)
     together = LANES // (LEND * (page // 4))
 
-    @pl.loop(0, read(plan, COUNT, base))
-    def _(block):
-        first_item = base + block * UNROLL
-        items = [item(plan, first_item + u, heads) for u in range(UNROLL)]
-        ropes = []
+    def work(read):
+        todo = [(read(ROW, u), [read(k, u) for k in range(LEND)]) for u in range(UNROLL)]
         for first in range(0, UNROLL, together):
-            ropes += rope_scores(queries, rope_keys, items[first : first + together], lanes, heads)
-        for first in range(0, UNROLL, PAIR):
-            mains = latent_scores(queries, pool, items[first : first + PAIR], heads)
-            for u, main in enumerate(mains, first):
-                start = pl.multiple_of(read(plan, SCORE_ROW, first_item + u), heads)
-                scores[pl.ds(start, heads), :] = jnp.where(
-                    position < read(plan, LIVE, first_item + u), (main + ropes[u]) * scale, FAR
-                )
+            ropes = list(
+                rope_scores(queries, rope_keys, todo[first : first + together], lanes, heads)
+            )
+            for k in range(first, first + together, PAIR):
+                mains = latent_scores(queries, pool, todo[k : k + PAIR], heads)
+                for u, main in enumerate(mains, k):
+                    start = pl.multiple_of(read(SCORE_ROW, u), heads)
+                    scores[pl.ds(start, heads), :] = jnp.where(
+                        position < read(LIVE, u), (main + ropes[u - first]) * scale, FAR
+                    )
+
+    each_block(plan, items, copies, base, work)
 
 
 def soften(scores, weights, norm, lse, total_rows):
     pitch = total_rows + (scores.shape[0] % total_rows) // (scores.shape[0] // total_rows)
     units = scores.shape[0] // pitch
-    step = 64
+    step = 128 if units == 1 else 32
     for r in range(0, total_rows, step):
         block = [scores[j * pitch + r : j * pitch + r + step, :] for j in range(units)]
         top = block[0]
@@ -273,27 +304,25 @@
             weights[j * pitch + r : j * pitch + r + step, :] = rounded
             total = total + rounded
         total = jnp.sum(total, axis=-1, keepdims=True)
-        norm[r : r + step, :] = jnp.broadcast_to(1.0 / total, (step, LANES))
+        scale = jnp.where(peak > FAR / 2, 1.0 / total, 0.0)
+        norm[r : r + step, :] = jnp.broadcast_to(scale, (step, LANES))
         lse[r : r + step, :] = jnp.broadcast_to(peak + jnp.log(total), (step, LANES))
 
 
-def value_work(pool, weights, context, plan, base, heads, add):
-    @pl.loop(0, read(plan, COUNT, base))
-    def _(block):
+def value_work(pool, weights, context, plan, items, copies, base, heads, add):
+    def work(read):
         for first in range(0, UNROLL, PAIR):
             starts, left, values = [], [], []
             for u in range(first, first + PAIR):
-                at = base + block * UNROLL + u
-                start, slots = item(plan, at, heads)
-                starts.append(start)
-                mine = weights[pl.ds(pl.multiple_of(read(plan, SCORE_ROW, at), heads), heads), :]
+                starts.append(read(ROW, u))
+                mine = weights[pl.ds(pl.multiple_of(read(SCORE_ROW, u), heads), heads), :]
                 none = jnp.zeros_like(mine)
                 left.append(
                     jnp.concatenate(
                         [mine if k == u - first else none for k in range(PAIR)], axis=1
                     )
                 )
-                values += [pool[s] for s in slots]
+                values += [pool[read(k, u)] for k in range(LEND)]
             summed = jnp.dot(
                 jnp.concatenate(left, axis=0).astype(jnp.bfloat16),
                 jnp.concatenate(values, axis=0),
@@ -306,16 +335,24 @@
                         part = part + context[c, pl.ds(start, heads), :]
                     context[c, pl.ds(start, heads), :] = part
 
+    each_block(plan, items, copies, base, work)
+
 
 def head_outs(context, norm, w_uv, rows, heads):
     width = w_uv.shape[2]
     for h in range(0, heads, 2):
         pair = []
         for k in range(2):
-            at = pl.ds(h + k, rows, stride=heads)
-            scale = norm[at, :]
+            scale = norm[pl.ds(h + k, rows, stride=heads), :]
+            at = pl.ds(h + k, rows, stride=heads + 1)
             pair.append(
-                jnp.concatenate([context[c, at, :] * scale for c in range(context.shape[0])], axis=1)
+                jnp.concatenate(
+                    [
+                        jnp.where(scale > 0.0, context[c, at, :] * scale, 0.0)
+                        for c in range(context.shape[0])
+                    ],
+                    axis=1,
+                )
             )
         both = jnp.dot(
             jnp.concatenate(pair, axis=0).astype(jnp.bfloat16),
@@ -366,9 +403,7 @@
             rows_of = spread[pl.ds(s * spacing + side, pieces // 2, stride=2), :]
             rope_keys[s, :, side * LANES : (side + 1) * LANES] = rows_of.astype(jnp.bfloat16)
     project_queries(message, w_uk, queries, heads, latent, narrow)
-    for copy in table:
-        copy.wait()
-    score_work(queries, pool, rope_keys, scores, plan, 0, heads, scale)
+    score_work(queries, pool, rope_keys, scores, plan, None, table, 0, heads, scale)
     soften(scores, weights, norm, lse, rows * heads)
 
 
@@ -379,9 +414,7 @@
     table = fetch_rows(items, plan, plan_sem)
     context[...] = jnp.zeros_like(context)
     logs[...] = heads_in_lanes(lse, rows, heads)
-    for copy in table:
-        copy.wait()
-    value_work(pool, weights, context, plan, 0, heads, True)
+    value_work(pool, weights, context, plan, items, table, 0, heads, True)
     width = w_uv.shape[2]
     for h, out in head_outs(context, norm, w_uv, rows, heads):
         outs[:, h * width : (h + 1) * width] = out
@@ -399,13 +432,10 @@
     asked = message[0:FIELDS, message.shape[1] - LANES :].astype(jnp.float32)
     items[...] = to_table(asked, asked[COUNT : COUNT + 1, :], rows, heads)
     table = fetch_rows(items, plan, plan_sem)
-    context[...] = jnp.zeros_like(context)
     project_queries(message, w_uk, queries, heads, latent, narrow)
-    for copy in table:
-        copy.wait()
-    score_work(queries, pool, rope_keys, scores, plan, base, heads, scale)
+    score_work(queries, pool, rope_keys, scores, plan, items, table, base, heads, scale)
     soften(scores, weights, norm, lse, rows * heads)
-    value_work(pool, weights, context, plan, base, heads, False)
+    value_work(pool, weights, context, plan, None, (), base, heads, False)
     width = w_uv.shape[2]
     lane = lax.broadcasted_iota(jnp.int32, (rows, LANES), 1)
     for h, out in head_outs(context, norm, w_uv, rows, heads):
@@ -490,15 +520,22 @@
     sem = pltpu.SemaphoreType.DMA
     stats = (rows * heads, LANES)
     padded = (rows + 1) * heads
-    block = pltpu.VMEM((tiles + 2, padded, LANES), f32)
-    contexts = pltpu.VMEM((tiles, padded, LANES), f32)
+    pitched = -(-(rows + 1) * (heads + 1) // 8) * 8
+    block = pltpu.VMEM((tiles + 2, pitched, LANES), f32)
+    contexts = pltpu.VMEM((tiles, pitched, LANES), f32)
     plan = pltpu.SMEM((TABLE_ROWS * LANES,), i32)
 
     message, own = call(
         pack_kernel,
         (shape((rows, heads * nope + narrow + LANES), bf16), shape((FIELDS, LANES), i32)),
-        [vmem()] * 5,
-        [pltpu.VMEM((FIELDS, LANES), f32)],
+        [pl.BlockSpec(memory_space=pl.ANY)] * 5,
+        [
+            pltpu.VMEM((1, rows), i32),
+            pltpu.VMEM((most, rows), i32),
+            pltpu.VMEM((2, rows), i32),
+            pltpu.VMEM((FIELDS, LANES), f32),
+            sem((5,)),
+        ],
         4,
         pl.CostEstimate(flops=20 * 10**9, bytes_accessed=64 * MIB, transcendentals=10**7),
         page=page,

time: 28.4 us -> 28.1 us (0.989)
  Pallas kernels: 13.1 us -> 12.8 us
  transfers between devices with their start and end apart: 5 -> 5, of which waited for: 2 -> 2; matrix products, arithmetic and copies ran while one was open for 0% -> 0% of each run, Pallas kernels for 40% -> 39%
where the time goes in v3:
time: 28.1 us; the launch traced here: 27.9 us
  Pallas kernels  12.8 us (46%)
  starting transfers between devices  9.15 us (33%)
  waiting for transfers between devices  5.24 us (19%)
  other arithmetic  0.64 us (2%)
    ppermute x5, starting transfers between devices, swap(): return lax.ppermute(block, axis, pairs)  9.15 us
    ppermute x5, waiting for transfers between devices, swap(): return lax.ppermute(block, axis, pairs)  5.24 us
    pallas_call x2, Pallas kernels, serve(): call(serve_kernel, shape((rows, heads * width + LANES), bf16), [vmem()] *...  4.64 us
    pallas_call x1, Pallas kernels, shards(): call(own_scores_kernel, (shape((slots, page // 4, 2 * LANES), bf16), shap...  3.58 us
    pallas_call x1, Pallas kernels, shards(): call(own_values_kernel, (shape((rows, heads * width), f32), shape((rows,...  2.23 us
    pallas_call x1, Pallas kernels, shards(): call(pack_kernel, (shape((rows, heads * nope + narrow + LANES), bf16), sh...  1.27 us
    convert_element_type x1, other arithmetic, shards(): return (kept + arrived.astype(f32)).astype(bf16)  0.64 us
    pallas_call x1, Pallas kernels, shards(): call(join_kernel, (shape((rows, cols), bf16), shape((rows, heads * width)...  0.6 us
  transfers between devices with their start and end apart: 5, of which 2 were waited for; matrix products, arithmetic and copies ran while one was open for 0% of the time, Pallas kernels for 39%

profile of v3, /device:TPU:0, one launch (start us, length us, event | category | flops | bytes accessed | tf_op | source)
XLA Modules:
  0.0 27.9 jit_solution(10975889411987452392)
XLA Ops:
  0.0 0.0 copy-start
  0.0 0.0 copy-start.3
  0.0 0.0 copy-start.4
  0.0 1.3 %shard_map.100 = (bf16[32,1664]{1,0:T(8,128)(2,1)S(1)}, s32[16,128]{1,0:T(8,128)S(1)}) custom-call(s32[1,32]{1,0:T(1,128)} %bitcast.5, s32[8,32]{1,0:T(8,128)} %bitcast.3, s32[2,32]{1,0:T(2,128)} %bitcast.4, bf16[32,1024]{1,0:T(8,128)(2,1)} %q_nope.1, bf16[32,512]{1,0:T(8,128)(2,1)} %q_rope.1), custom_call_target="tpu_custom_call" | custom-call | flops 20000000000 | bytes 67108864 | tf_op jit(solution)/shard_map/pallas_call | solution.py:528
  1.3 0.0 copy-start.2
  1.3 0.6 %collective-permute-start = (bf16[32,1664]{1,0:T(8,128)(2,1)S(1)}, bf16[32,1664]{1,0:T(8,128)(2,1)S(1)}, u32[]{:S(2)}, u32[]{:S(2)}) collective-permute-start(bf16[32,1664]{1,0:T(8,128)(2,1)S(1)} %get-tuple-element.17.message), channel_id=1, source_target_pairs={{0,2},{2,0},{4,6},{6,4},{8,10},{10,8},{12,14},{14,12},{16,18},{18,... | collective-permute-start | bytes 319496 | tf_op jit(solution)/shard_map/ppermute | solution.py:30
  1.9 5.6 %collective-permute-start.2 = (bf16[32,1664]{1,0:T(8,128)(2,1)S(1)}, bf16[32,1664]{1,0:T(8,128)(2,1)S(1)}, u32[]{:S(2)}, u32[]{:S(2)}) collective-permute-start(bf16[32,1664]{1,0:T(8,128)(2,1)S(1)} %get-tuple-element.17.message), channel_id=1, source_target_pairs={{2,4},{4,2},{6,8},{8,6},{10,12},{12,10},{14,16},{16,14},{18,20},{2... | collective-permute-start | bytes 319496 | tf_op jit(solution)/shard_map/ppermute | solution.py:30
  7.5 0.0 copy-done
  7.5 0.0 copy-done.3
  7.5 0.0 copy-done.4
  7.5 3.6 %shard_map.101 = (bf16[96,16,256]{2,1,0:T(8,128)(2,1)S(1)}, f32[1056,128]{1,0:T(8,128)S(1)}, f32[256,128]{1,0:T(8,128)S(1)}, f32[256,128]{1,0:T(8,128)S(1)}, s32[16,128]{1,0:T(8,128)S(1)}) custom-call(s32[16,128]{1,0:T(8,128)S(1)} %get-tuple-element.16.own, bf16[32,1664]{1,0:T(8,128)(2,1)S(1)} %get-tuple-element.17.message, bf16[96,4096]{1,0:T(8,128)(2,1)S(1)} %copy-done.4, ...), custom_call_target="tpu_custom_call" | custom-call | flops 167772160 | bytes 7864320 | tf_op jit(solution)/shard_map/pallas_call | solution.py:546
  11.1 0.0 collective-permute-done.message
  11.1 0.0 copy-done.2
  11.1 2.0 %shard_map.103 = bf16[32,1152]{1,0:T(8,128)(2,1)S(1)} custom-call(bf16[32,1664]{1,0:T(8,128)(2,1)S(1)} %collective-permute-done.message, bf16[96,64,512]{2,1,0:T(8,128)(2,1)S(1)} %copy-done, bf16[96,16,256]{2,1,0:T(8,128)(2,1)S(1)} %get-tuple-element.24.rope_keys, bf16[8,128,512]{2,1,0:T(8,128)(2,1)S(1)} %copy-done.3, bf16[8,512,128]{2,1,0:T(8,128)(2,1)S(1)} %copy-done.2), custom_call_target="tpu_custom_call" | custom-call | tf_op jit(solution)/shard_map/pallas_call | solution.py:588
  13.1 0.1 collective-permute-start.1
  13.2 0.0 collective-permute-done.2.message
  13.2 2.7 %shard_map.104 = bf16[32,1152]{1,0:T(8,128)(2,1)S(1)} custom-call(bf16[32,1664]{1,0:T(8,128)(2,1)S(1)} %collective-permute-done.2.message, bf16[96,64,512]{2,1,0:T(8,128)(2,1)S(1)} %copy-done, bf16[96,16,256]{2,1,0:T(8,128)(2,1)S(1)} %get-tuple-element.24.rope_keys, bf16[8,128,512]{2,1,0:T(8,128)(2,1)S(1)} %copy-done.3, bf16[8,512,128]{2,1,0:T(8,128)(2,1)S(1)} %copy-done.2), custom_call_target="tpu_custom_call" | custom-call | tf_op jit(solution)/shard_map/pallas_call | solution.py:588
  15.8 0.0 copy-start.1
  15.9 1.4 %collective-permute-start.3 = (bf16[32,1152]{1,0:T(8,128)(2,1)S(1)}, bf16[32,1152]{1,0:T(8,128)(2,1)S(1)}, u32[]{:S(2)}, u32[]{:S(2)}) collective-permute-start(bf16[32,1152]{1,0:T(8,128)(2,1)S(1)} %shard_map.104), channel_id=1, source_target_pairs={{2,4},{4,2},{6,8},{8,6},{10,12},{12,10},{14,16},{16,14},{18,20},{2... | collective-permute-start | bytes 221192 | tf_op jit(solution)/shard_map/ppermute | solution.py:30
  17.2 2.2 %shard_map.102 = (f32[32,1024]{1,0:T(8,128)S(1)}, f32[32,128]{1,0:T(8,128)S(1)}) custom-call(s32[16,128]{1,0:T(8,128)S(1)} %get-tuple-element.18.items, bf16[96,64,512]{2,1,0:T(8,128)(2,1)S(1)} %copy-done, f32[1056,128]{1,0:T(8,128)S(1)} %get-tuple-element.19.weights, f32[256,128]{1,0:T(8,128)S(1)} %get-tuple-element.20.norm, ...), custom_call_target="tpu_custom_call" | custom-call | tf_op jit(solution)/shard_map/pallas_call | solution.py:602
  19.5 0.0 collective-permute-done.1.from_a
  19.5 2.9 %collective-permute-done.3.from_b = bf16[32,1152]{1,0:T(8,128)(2,1)S(1)} collective-permute-done((bf16[32,1152]{1,0:T(8,128)(2,1)S(1)}, bf16[32,1152]{1,0:T(8,128)(2,1)S(1)}, u32[]{:S(2)}, u32[]{:S(2)}) %collective-permute-start.3) | collective-permute-done | bytes 73760 | tf_op jit(solution)/shard_map/ppermute | solution.py:30
  22.4 0.0 copy-done.1
  22.4 0.6 %shard_map.105 = (bf16[32,1024]{1,0:T(8,128)(2,1)S(1)}, bf16[32,1024]{1,0:T(8,128)(2,1)S(1)}) custom-call(f32[32,1024]{1,0:T(8,128)S(1)} %get-tuple-element.22.outs, f32[32,128]{1,0:T(8,128)S(1)} %get-tuple-element.23.logs, bf16[32,1152]{1,0:T(8,128)(2,1)S(1)} %collective-permute-done.1.from_a, bf16[32,1152]{1,0:T(8,128)(2,1)S(1)} %collective-permute-done.3.from_b, ...), custom_call_target="tpu_custom_call" | custom-call | tf_op jit(solution)/shard_map/pallas_call | solution.py:611
  23.0 1.5 %collective-permute-start.4 = (bf16[32,1024]{1,0:T(8,128)(2,1)S(1)}, bf16[32,1024]{1,0:T(8,128)(2,1)S(1)}, u32[]{:S(2)}, u32[]{:S(2)}) collective-permute-start(bf16[32,1024]{1,0:T(8,128)(2,1)S(1)} %get-tuple-element.26), channel_id=1, source_target_pairs={{0,1},{1,0},{2,3},{3,2},{4,5},{5,4},{6,7},{7,6},{8,9},{9,8},{10,11... | collective-permute-start | bytes 196616 | tf_op jit(solution)/shard_map/ppermute | solution.py:30
  24.5 0.5 %shard_map.106 = f32[32,1024]{1,0:T(8,128)S(1)} custom-call(bf16[32,1024]{1,0:T(8,128)(2,1)S(1)} %get-tuple-element.25.joined, bf16[1024,2048]{1,0:T(8,128)(2,1)S(1)} %copy-done.1), custom_call_target="tpu_custom_call" | custom-call | tf_op jit(solution)/shard_map/pallas_call | solution.py:620
  25.0 2.3 %collective-permute-done.4 = bf16[32,1024]{1,0:T(8,128)(2,1)S(1)} collective-permute-done((bf16[32,1024]{1,0:T(8,128)(2,1)S(1)}, bf16[32,1024]{1,0:T(8,128)(2,1)S(1)}, u32[]{:S(2)}, u32[]{:S(2)}) %collective-permute-start.4) | collective-permute-done | bytes 65568 | tf_op jit(solution)/shard_map/ppermute | solution.py:30
  27.3 0.6 %add_convert_fusion = bf16[32,1024]{1,0:T(8,128)(2,1)} fusion(f32[32,1024]{1,0:T(8,128)S(1)} %shard_map.106, bf16[32,1024]{1,0:T(8,128)(2,1)S(1)} %collective-permute-done.4), kind=kLoop, calls=%fused_computation | loop fusion | flops 98304 | bytes 262144 | tf_op jit(solution)/shard_map/convert_element_type | solution.py:621
Async XLA Ops:
  0.0 7.5 %copy-start = (bf16[96,64,512]{2,1,0:T(8,128)(2,1)S(1)}, bf16[96,64,512]{2,1,0:T(8,128)(2,1)}, u32[]{:S(2)}) copy-start(bf16[96,64,512]{2,1,0:T(8,128)(2,1)} %pool.7) | copy-start | bytes 18874372
  0.0 7.5 %copy-start.3 = (bf16[8,128,512]{2,1,0:T(8,128)(2,1)S(1)}, bf16[8,128,512]{2,1,0:T(8,128)(2,1)}, u32[]{:S(2)}) copy-start(bf16[8,128,512]{2,1,0:T(8,128)(2,1)} %w_uk.5) | copy-start | bytes 3145732
  0.0 7.5 %copy-start.4 = (bf16[96,4096]{1,0:T(8,128)(2,1)S(1)}, bf16[96,4096]{1,0:T(8,128)(2,1)}, u32[]{:S(2)}) copy-start(bf16[96,4096]{1,0:T(8,128)(2,1)} %rope_pages.1) | copy-start | bytes 2359300
  1.3 9.8 %copy-start.2 = (bf16[8,512,128]{2,1,0:T(8,128)(2,1)S(1)}, bf16[8,512,128]{2,1,0:T(8,128)(2,1)}, u32[]{:S(2)}) copy-start(bf16[8,512,128]{2,1,0:T(8,128)(2,1)} %w_uv.5) | copy-start | bytes 3145732
  1.3 9.8 %collective-permute-start = (bf16[32,1664]{1,0:T(8,128)(2,1)S(1)}, bf16[32,1664]{1,0:T(8,128)(2,1)S(1)}, u32[]{:S(2)}, u32[]{:S(2)}) collective-permute-start(bf16[32,1664]{1,0:T(8,128)(2,1)S(1)} %get-tuple-element.17.message), channel_id=1, source_target_pairs={{0,2},{2,0},{4,6},{6,4},{8,10},{10,8},{12,14},{14,12},{16,18},{18,... | collective-permute-start | bytes 319496 | tf_op jit(solution)/shard_map/ppermute | solution.py:30
  1.9 11.3 %collective-permute-start.2 = (bf16[32,1664]{1,0:T(8,128)(2,1)S(1)}, bf16[32,1664]{1,0:T(8,128)(2,1)S(1)}, u32[]{:S(2)}, u32[]{:S(2)}) collective-permute-start(bf16[32,1664]{1,0:T(8,128)(2,1)S(1)} %get-tuple-element.17.message), channel_id=1, source_target_pairs={{2,4},{4,2},{6,8},{8,6},{10,12},{12,10},{14,16},{16,14},{18,20},{2... | collective-permute-start | bytes 319496 | tf_op jit(solution)/shard_map/ppermute | solution.py:30
  13.1 6.4 %collective-permute-start.1 = (bf16[32,1152]{1,0:T(8,128)(2,1)S(1)}, bf16[32,1152]{1,0:T(8,128)(2,1)S(1)}, u32[]{:S(2)}, u32[]{:S(2)}) collective-permute-start(bf16[32,1152]{1,0:T(8,128)(2,1)S(1)} %shard_map.103), channel_id=1, source_target_pairs={{0,2},{2,0},{4,6},{6,4},{8,10},{10,8},{12,14},{14,12},{16,18},{18,... | collective-permute-start | bytes 221192 | tf_op jit(solution)/shard_map/ppermute | solution.py:30
  15.8 6.6 %copy-start.1 = (bf16[1024,2048]{1,0:T(8,128)(2,1)S(1)}, bf16[1024,2048]{1,0:T(8,128)(2,1)}, u32[]{:S(2)}) copy-start(bf16[1024,2048]{1,0:T(8,128)(2,1)} %w_o.3) | copy-start | bytes 12582916
  15.9 6.5 %collective-permute-start.3 = (bf16[32,1152]{1,0:T(8,128)(2,1)S(1)}, bf16[32,1152]{1,0:T(8,128)(2,1)S(1)}, u32[]{:S(2)}, u32[]{:S(2)}) collective-permute-start(bf16[32,1152]{1,0:T(8,128)(2,1)S(1)} %shard_map.104), channel_id=1, source_target_pairs={{2,4},{4,2},{6,8},{8,6},{10,12},{12,10},{14,16},{16,14},{18,20},{2... | collective-permute-start | bytes 221192 | tf_op jit(solution)/shard_map/ppermute | solution.py:30
  23.0 4.3 %collective-permute-start.4 = (bf16[32,1024]{1,0:T(8,128)(2,1)S(1)}, bf16[32,1024]{1,0:T(8,128)(2,1)S(1)}, u32[]{:S(2)}, u32[]{:S(2)}) collective-permute-start(bf16[32,1024]{1,0:T(8,128)(2,1)S(1)} %get-tuple-element.26), channel_id=1, source_target_pairs={{0,1},{1,0},{2,3},{3,2},{4,5},{5,4},{6,7},{7,6},{8,9},{9,8},{10,11... | collective-permute-start | bytes 196616 | tf_op jit(solution)/shard_map/ppermute | solution.py:30

commit v4 on v3

--- a/solution.py
+++ b/solution.py
@@ -15,8 +15,9 @@
 ROW, LIVE, COUNT, SCORE_ROW = 2, 3, 4, 5
 TABLE_ROWS = 6
 FAR = -1e30
-UNROLL = 8
+UNROLL = 16
 PAIR = 2
+QUAD = 1
 MIB = 1 << 20
 
 
@@ -340,12 +341,12 @@
 
 def head_outs(context, norm, w_uv, rows, heads):
     width = w_uv.shape[2]
-    for h in range(0, heads, 2):
-        pair = []
-        for k in range(2):
-            scale = norm[pl.ds(h + k, rows, stride=heads), :]
-            at = pl.ds(h + k, rows, stride=heads + 1)
-            pair.append(
+    for first in range(0, heads, QUAD):
+        left = []
+        for h in range(first, first + QUAD):
+            scale = norm[pl.ds(h, rows, stride=heads), :]
+            at = pl.ds(h, rows, stride=heads + 1)
+            left.append(
                 jnp.concatenate(
                     [
                         jnp.where(scale > 0.0, context[c, at, :] * scale, 0.0)
@@ -354,13 +355,13 @@
                     axis=1,
                 )
             )
-        both = jnp.dot(
-            jnp.concatenate(pair, axis=0).astype(jnp.bfloat16),
-            jnp.concatenate([w_uv[h], w_uv[h + 1]], axis=1),
+        found = jnp.dot(
+            jnp.concatenate(left, axis=0).astype(jnp.bfloat16),
+            jnp.concatenate([w_uv[h] for h in range(first, first + QUAD)], axis=1),
             preferred_element_type=jnp.float32,
         )
-        yield h, both[:rows, :width]
-        yield h + 1, both[rows:, width:]
+        for k in range(QUAD):
+            yield first + k, found[k * rows : (k + 1) * rows, k * width : (k + 1) * width]
 
 
 def heads_in_lanes(lse, rows, heads):

time: 28.1 us -> 28.4 us (1.011)
  starting transfers between devices: 9.15 us -> 9.8 us
  waiting for transfers between devices: 5.24 us -> 4.67 us
    ppermute x5, starting transfers between devices: 9.15 us -> 9.8 us  [swap(): return lax.ppermute(block, axis, pairs)]
    ppermute x5, waiting for transfers between devices: 5.24 us -> 4.67 us  [swap(): return lax.ppermute(block, axis, pairs)]
where the time goes in v4:
time: 28.4 us; the launch traced here: 28.3 us
  Pallas kernels  13 us (46%)
  starting transfers between devices  9.8 us (35%)
  waiting for transfers between devices  4.67 us (16%)
  other arithmetic  0.64 us (2%)
    ppermute x5, starting transfers between devices, swap(): return lax.ppermute(block, axis, pairs)  9.8 us
    pallas_call x2, Pallas kernels, serve(): call(serve_kernel, shape((rows, heads * width + LANES), bf16), [vmem()] *...  4.91 us
    ppermute x5, waiting for transfers between devices, swap(): return lax.ppermute(block, axis, pairs)  4.67 us
    pallas_call x1, Pallas kernels, shards(): call(own_scores_kernel, (shape((slots, page // 4, 2 * LANES), bf16), shap...  3.65 us
    pallas_call x1, Pallas kernels, shards(): call(own_values_kernel, (shape((rows, heads * width), f32), shape((rows,...  2.14 us
    pallas_call x1, Pallas kernels, shards(): call(pack_kernel, (shape((rows, heads * nope + narrow + LANES), bf16), sh...  1.27 us
    convert_element_type x1, other arithmetic, shards(): return (kept + arrived.astype(f32)).astype(bf16)  0.64 us
    pallas_call x1, Pallas kernels, shards(): call(join_kernel, (shape((rows, cols), bf16), shape((rows, heads * width)...  0.59 us
  transfers between devices with their start and end apart: 5, of which 2 were waited for; matrix products, arithmetic and copies ran while one was open for 0% of the time, Pallas kernels for 39%

profile of v4, /device:TPU:0, one launch (start us, length us, event | category | flops | bytes accessed | tf_op | source)
XLA Modules:
  0.0 28.3 jit_solution(16498744939098948163)
XLA Ops:
  0.0 0.0 copy-start
  0.0 0.0 copy-start.3
  0.0 0.0 copy-start.4
  0.0 1.3 %shard_map.100 = (bf16[32,1664]{1,0:T(8,128)(2,1)S(1)}, s32[16,128]{1,0:T(8,128)S(1)}) custom-call(s32[1,32]{1,0:T(1,128)} %bitcast.5, s32[8,32]{1,0:T(8,128)} %bitcast.3, s32[2,32]{1,0:T(2,128)} %bitcast.4, bf16[32,1024]{1,0:T(8,128)(2,1)} %q_nope.1, bf16[32,512]{1,0:T(8,128)(2,1)} %q_rope.1), custom_call_target="tpu_custom_call" | custom-call | flops 20000000000 | bytes 67108864 | tf_op jit(solution)/shard_map/pallas_call | solution.py:529
  1.3 0.0 copy-start.2
  1.3 0.6 %collective-permute-start = (bf16[32,1664]{1,0:T(8,128)(2,1)S(1)}, bf16[32,1664]{1,0:T(8,128)(2,1)S(1)}, u32[]{:S(2)}, u32[]{:S(2)}) collective-permute-start(bf16[32,1664]{1,0:T(8,128)(2,1)S(1)} %get-tuple-element.17.message), channel_id=1, source_target_pairs={{0,2},{2,0},{4,6},{6,4},{8,10},{10,8},{12,14},{14,12},{16,18},{18,... | collective-permute-start | bytes 319496 | tf_op jit(solution)/shard_map/ppermute | solution.py:31
  1.9 5.6 %collective-permute-start.2 = (bf16[32,1664]{1,0:T(8,128)(2,1)S(1)}, bf16[32,1664]{1,0:T(8,128)(2,1)S(1)}, u32[]{:S(2)}, u32[]{:S(2)}) collective-permute-start(bf16[32,1664]{1,0:T(8,128)(2,1)S(1)} %get-tuple-element.17.message), channel_id=1, source_target_pairs={{2,4},{4,2},{6,8},{8,6},{10,12},{12,10},{14,16},{16,14},{18,20},{2... | collective-permute-start | bytes 319496 | tf_op jit(solution)/shard_map/ppermute | solution.py:31
  7.5 0.0 copy-done
  7.5 0.0 copy-done.3
  7.5 0.0 copy-done.4
  7.5 3.6 %shard_map.101 = (bf16[96,16,256]{2,1,0:T(8,128)(2,1)S(1)}, f32[1056,128]{1,0:T(8,128)S(1)}, f32[256,128]{1,0:T(8,128)S(1)}, f32[256,128]{1,0:T(8,128)S(1)}, s32[16,128]{1,0:T(8,128)S(1)}) custom-call(s32[16,128]{1,0:T(8,128)S(1)} %get-tuple-element.16.own, bf16[32,1664]{1,0:T(8,128)(2,1)S(1)} %get-tuple-element.17.message, bf16[96,4096]{1,0:T(8,128)(2,1)S(1)} %copy-done.4, ...), custom_call_target="tpu_custom_call" | custom-call | flops 167772160 | bytes 7864320 | tf_op jit(solution)/shard_map/pallas_call | solution.py:547
  11.2 0.0 collective-permute-done.message
  11.2 0.0 copy-done.2
  11.2 2.5 %shard_map.103 = bf16[32,1152]{1,0:T(8,128)(2,1)S(1)} custom-call(bf16[32,1664]{1,0:T(8,128)(2,1)S(1)} %collective-permute-done.message, bf16[96,64,512]{2,1,0:T(8,128)(2,1)S(1)} %copy-done, bf16[96,16,256]{2,1,0:T(8,128)(2,1)S(1)} %get-tuple-element.24.rope_keys, bf16[8,128,512]{2,1,0:T(8,128)(2,1)S(1)} %copy-done.3, bf16[8,512,128]{2,1,0:T(8,128)(2,1)S(1)} %copy-done.2), custom_call_target="tpu_custom_call" | custom-call | tf_op jit(solution)/shard_map/pallas_call | solution.py:589
  13.6 0.1 collective-permute-start.1
  13.7 0.0 collective-permute-done.2.message
  13.7 2.5 %shard_map.104 = bf16[32,1152]{1,0:T(8,128)(2,1)S(1)} custom-call(bf16[32,1664]{1,0:T(8,128)(2,1)S(1)} %collective-permute-done.2.message, bf16[96,64,512]{2,1,0:T(8,128)(2,1)S(1)} %copy-done, bf16[96,16,256]{2,1,0:T(8,128)(2,1)S(1)} %get-tuple-element.24.rope_keys, bf16[8,128,512]{2,1,0:T(8,128)(2,1)S(1)} %copy-done.3, bf16[8,512,128]{2,1,0:T(8,128)(2,1)S(1)} %copy-done.2), custom_call_target="tpu_custom_call" | custom-call | tf_op jit(solution)/shard_map/pallas_call | solution.py:589
  16.2 0.0 copy-start.1
  16.2 2.0 %collective-permute-start.3 = (bf16[32,1152]{1,0:T(8,128)(2,1)S(1)}, bf16[32,1152]{1,0:T(8,128)(2,1)S(1)}, u32[]{:S(2)}, u32[]{:S(2)}) collective-permute-start(bf16[32,1152]{1,0:T(8,128)(2,1)S(1)} %shard_map.104), channel_id=1, source_target_pairs={{2,4},{4,2},{6,8},{8,6},{10,12},{12,10},{14,16},{16,14},{18,20},{2... | collective-permute-start | bytes 221192 | tf_op jit(solution)/shard_map/ppermute | solution.py:31
  18.2 2.1 %shard_map.102 = (f32[32,1024]{1,0:T(8,128)S(1)}, f32[32,128]{1,0:T(8,128)S(1)}) custom-call(s32[16,128]{1,0:T(8,128)S(1)} %get-tuple-element.18.items, bf16[96,64,512]{2,1,0:T(8,128)(2,1)S(1)} %copy-done, f32[1056,128]{1,0:T(8,128)S(1)} %get-tuple-element.19.weights, f32[256,128]{1,0:T(8,128)S(1)} %get-tuple-element.20.norm, ...), custom_call_target="tpu_custom_call" | custom-call | tf_op jit(solution)/shard_map/pallas_call | solution.py:603
  20.4 0.0 collective-permute-done.1.from_a
  20.4 2.4 %collective-permute-done.3.from_b = bf16[32,1152]{1,0:T(8,128)(2,1)S(1)} collective-permute-done((bf16[32,1152]{1,0:T(8,128)(2,1)S(1)}, bf16[32,1152]{1,0:T(8,128)(2,1)S(1)}, u32[]{:S(2)}, u32[]{:S(2)}) %collective-permute-start.3) | collective-permute-done | bytes 73760 | tf_op jit(solution)/shard_map/ppermute | solution.py:31
  22.7 0.0 copy-done.1
  22.7 0.6 %shard_map.105 = (bf16[32,1024]{1,0:T(8,128)(2,1)S(1)}, bf16[32,1024]{1,0:T(8,128)(2,1)S(1)}) custom-call(f32[32,1024]{1,0:T(8,128)S(1)} %get-tuple-element.22.outs, f32[32,128]{1,0:T(8,128)S(1)} %get-tuple-element.23.logs, bf16[32,1152]{1,0:T(8,128)(2,1)S(1)} %collective-permute-done.1.from_a, bf16[32,1152]{1,0:T(8,128)(2,1)S(1)} %collective-permute-done.3.from_b, ...), custom_call_target="tpu_custom_call" | custom-call | tf_op jit(solution)/shard_map/pallas_call | solution.py:612
  23.3 1.5 %collective-permute-start.4 = (bf16[32,1024]{1,0:T(8,128)(2,1)S(1)}, bf16[32,1024]{1,0:T(8,128)(2,1)S(1)}, u32[]{:S(2)}, u32[]{:S(2)}) collective-permute-start(bf16[32,1024]{1,0:T(8,128)(2,1)S(1)} %get-tuple-element.26), channel_id=1, source_target_pairs={{0,1},{1,0},{2,3},{3,2},{4,5},{5,4},{6,7},{7,6},{8,9},{9,8},{10,11... | collective-permute-start | bytes 196616 | tf_op jit(solution)/shard_map/ppermute | solution.py:31
  24.9 0.5 %shard_map.106 = f32[32,1024]{1,0:T(8,128)S(1)} custom-call(bf16[32,1024]{1,0:T(8,128)(2,1)S(1)} %get-tuple-element.25.joined, bf16[1024,2048]{1,0:T(8,128)(2,1)S(1)} %copy-done.1), custom_call_target="tpu_custom_call" | custom-call | tf_op jit(solution)/shard_map/pallas_call | solution.py:621
  25.3 2.3 %collective-permute-done.4 = bf16[32,1024]{1,0:T(8,128)(2,1)S(1)} collective-permute-done((bf16[32,1024]{1,0:T(8,128)(2,1)S(1)}, bf16[32,1024]{1,0:T(8,128)(2,1)S(1)}, u32[]{:S(2)}, u32[]{:S(2)}) %collective-permute-start.4) | collective-permute-done | bytes 65568 | tf_op jit(solution)/shard_map/ppermute | solution.py:31
  27.6 0.6 %add_convert_fusion = bf16[32,1024]{1,0:T(8,128)(2,1)} fusion(f32[32,1024]{1,0:T(8,128)S(1)} %shard_map.106, bf16[32,1024]{1,0:T(8,128)(2,1)S(1)} %collective-permute-done.4), kind=kLoop, calls=%fused_computation | loop fusion | flops 98304 | bytes 262144 | tf_op jit(solution)/shard_map/convert_element_type | solution.py:622
Async XLA Ops:
  0.0 7.5 %copy-start = (bf16[96,64,512]{2,1,0:T(8,128)(2,1)S(1)}, bf16[96,64,512]{2,1,0:T(8,128)(2,1)}, u32[]{:S(2)}) copy-start(bf16[96,64,512]{2,1,0:T(8,128)(2,1)} %pool.7) | copy-start | bytes 18874372
  0.0 7.5 %copy-start.3 = (bf16[8,128,512]{2,1,0:T(8,128)(2,1)S(1)}, bf16[8,128,512]{2,1,0:T(8,128)(2,1)}, u32[]{:S(2)}) copy-start(bf16[8,128,512]{2,1,0:T(8,128)(2,1)} %w_uk.5) | copy-start | bytes 3145732
  0.0 7.5 %copy-start.4 = (bf16[96,4096]{1,0:T(8,128)(2,1)S(1)}, bf16[96,4096]{1,0:T(8,128)(2,1)}, u32[]{:S(2)}) copy-start(bf16[96,4096]{1,0:T(8,128)(2,1)} %rope_pages.1) | copy-start | bytes 2359300
  1.3 9.9 %copy-start.2 = (bf16[8,512,128]{2,1,0:T(8,128)(2,1)S(1)}, bf16[8,512,128]{2,1,0:T(8,128)(2,1)}, u32[]{:S(2)}) copy-start(bf16[8,512,128]{2,1,0:T(8,128)(2,1)} %w_uv.5) | copy-start | bytes 3145732
  1.3 9.9 %collective-permute-start = (bf16[32,1664]{1,0:T(8,128)(2,1)S(1)}, bf16[32,1664]{1,0:T(8,128)(2,1)S(1)}, u32[]{:S(2)}, u32[]{:S(2)}) collective-permute-start(bf16[32,1664]{1,0:T(8,128)(2,1)S(1)} %get-tuple-element.17.message), channel_id=1, source_target_pairs={{0,2},{2,0},{4,6},{6,4},{8,10},{10,8},{12,14},{14,12},{16,18},{18,... | collective-permute-start | bytes 319496 | tf_op jit(solution)/shard_map/ppermute | solution.py:31
  1.9 11.9 %collective-permute-start.2 = (bf16[32,1664]{1,0:T(8,128)(2,1)S(1)}, bf16[32,1664]{1,0:T(8,128)(2,1)S(1)}, u32[]{:S(2)}, u32[]{:S(2)}) collective-permute-start(bf16[32,1664]{1,0:T(8,128)(2,1)S(1)} %get-tuple-element.17.message), channel_id=1, source_target_pairs={{2,4},{4,2},{6,8},{8,6},{10,12},{12,10},{14,16},{16,14},{18,20},{2... | collective-permute-start | bytes 319496 | tf_op jit(solution)/shard_map/ppermute | solution.py:31
  13.6 6.7 %collective-permute-start.1 = (bf16[32,1152]{1,0:T(8,128)(2,1)S(1)}, bf16[32,1152]{1,0:T(8,128)(2,1)S(1)}, u32[]{:S(2)}, u32[]{:S(2)}) collective-permute-start(bf16[32,1152]{1,0:T(8,128)(2,1)S(1)} %shard_map.103), channel_id=1, source_target_pairs={{0,2},{2,0},{4,6},{6,4},{8,10},{10,8},{12,14},{14,12},{16,18},{18,... | collective-permute-start | bytes 221192 | tf_op jit(solution)/shard_map/ppermute | solution.py:31
  16.2 6.6 %copy-start.1 = (bf16[1024,2048]{1,0:T(8,128)(2,1)S(1)}, bf16[1024,2048]{1,0:T(8,128)(2,1)}, u32[]{:S(2)}) copy-start(bf16[1024,2048]{1,0:T(8,128)(2,1)} %w_o.3) | copy-start | bytes 12582916
  16.2 6.5 %collective-permute-start.3 = (bf16[32,1152]{1,0:T(8,128)(2,1)S(1)}, bf16[32,1152]{1,0:T(8,128)(2,1)S(1)}, u32[]{:S(2)}, u32[]{:S(2)}) collective-permute-start(bf16[32,1152]{1,0:T(8,128)(2,1)S(1)} %shard_map.104), channel_id=1, source_target_pairs={{2,4},{4,2},{6,8},{8,6},{10,12},{12,10},{14,16},{16,14},{18,20},{2... | collective-permute-start | bytes 221192 | tf_op jit(solution)/shard_map/ppermute | solution.py:31
  23.3 4.3 %collective-permute-start.4 = (bf16[32,1024]{1,0:T(8,128)(2,1)S(1)}, bf16[32,1024]{1,0:T(8,128)(2,1)S(1)}, u32[]{:S(2)}, u32[]{:S(2)}) collective-permute-start(bf16[32,1024]{1,0:T(8,128)(2,1)S(1)} %get-tuple-element.26), channel_id=1, source_target_pairs={{0,1},{1,0},{2,3},{3,2},{4,5},{5,4},{6,7},{7,6},{8,9},{9,8},{10,11... | collective-permute-start | bytes 196616 | tf_op jit(solution)/shard_map/ppermute | solution.py:31
